TPU v7x, 32 devices: a whole 2x2x4 slice. The times are simulated.
32 devices in a mesh: dp: 8 (over z, x), tile: 4 (over y, core).
Axes of the slice: x: 2, y: 2, z: 4, core: 2. Of those that a mesh axis runs over, the one named last changes fastest.
Arguments:
- frames: bfloat16 [32, 4, 64, 256], P('dp', 'tile'), may hold values from -6 to 6
- kernels: bfloat16 [32, 9, 256, 256], P('dp'), may hold values from -0.125 to 0.125
- experts: int32 [32, 4, 4], P('dp', 'tile'), may hold values from 0 to 31, as said below
- counts: int32 [32, 4], P('dp', 'tile'), may hold values from 2 to 4
- gate_weights: float32 [32, 4, 4], P('dp', 'tile'), may hold values from 0.25 to 1
- cotangent: bfloat16 [32, 4, 64, 256], P('dp', 'tile'), may hold values from -6 to 6
Outputs:
- frames_out: bfloat16 [32, 4, 64, 256], P('dp', 'tile')
- input_grad: bfloat16 [32, 4, 64, 256], P('dp', 'tile')
- gate_grad: float32 [32, 4, 4], P('dp', 'tile')
- kernel_grad: float32 [32, 9, 256, 256], P('dp', None, None, 'tile')
Inputs may be any that keep to these rules, and one draw needn't show every extreme that they name: A tile's 4 experts have distinct values of id // 4. Among the 4 tiles of one device (frames d * 4 to (d + 1) * 4 - 1 at one tile index), each value of id // 4 is named by at most 2 tiles, by exactly 2 for some, and all its slots there name the same id. A tile uses its first counts slots; later slots are ignored.
All inputs are finite; a program needn't handle non-finite values.
Results may differ from a plain program's by a relative error of at most 0.005.
Values may be sent and summed in bfloat16 or wider, within the bound.
A program may use at most 256 MiB of HBM per device.

v0:
```python
import jax
import jax.numpy as jnp
from jax import lax
from jax.sharding import PartitionSpec as P

CAP = 2


highest = lax.Precision.HIGHEST


def padded(x, sides, width):
    for axis, dim in sides:
        count, length = (lax.axis_size(axis), x.shape[dim])
        up = [(i, (i + 1) % count) for i in range(count - 1)]
        down = [(j, i) for i, j in up]
        last = lax.slice_in_dim(x, length - width, length, axis=dim)
        initial = lax.slice_in_dim(x, 0, width, axis=dim)
        before = lax.ppermute(last, axis, up)
        after = lax.ppermute(initial, axis, down)
        x = jnp.concatenate([before, x, after], axis=dim)
    return x


def convolve(window, kernel_weight):
    number_of_rows = window.shape[0] - 2
    columns = window.shape[1]
    widened = jnp.pad(window, ((0, 0), (1, 1), (0, 0)))
    total = jnp.zeros((number_of_rows * columns, kernel_weight.shape[2]), jnp.float32)
    for row_off in range(3):
        for col_off in range(3):
            patch = widened[
                row_off : row_off + number_of_rows, col_off : col_off + columns
            ].reshape(number_of_rows * columns, -1)
            total = total + jnp.dot(
                patch, kernel_weight[3 * row_off + col_off], preferred_element_type=jnp.float32
            )
    return total.reshape(number_of_rows, columns, -1)


def transpose_conv(grad_out, kernel_weight):
    number_of_rows = grad_out.shape[0]
    columns = grad_out.shape[1]
    widened = jnp.pad(grad_out, ((2, 2), (1, 1), (0, 0)))
    total = jnp.zeros(((number_of_rows + 2) * columns, kernel_weight.shape[1]), jnp.float32)
    for row_off in range(3):
        for col_off in range(3):
            patch = widened[
                2 - row_off : 4 - row_off + number_of_rows, 2 - col_off : 2 - col_off + columns
            ].reshape((number_of_rows + 2) * columns, -1)
            total = total + lax.dot_general(
                patch,
                kernel_weight[3 * row_off + col_off],
                (((1,), (1,)), ((), ())),
                preferred_element_type=jnp.float32,
            )
    return total.reshape(number_of_rows + 2, columns, -1)


def activation(pre):
    squash = jax.nn.sigmoid(pre)
    return (pre * squash, squash * (1.0 + pre * (1.0 - squash)))


def owner_forward(inputs, expert_pick, item_filled, kernels):
    sources, capacity = (inputs.shape[0], inputs.shape[1])
    flat_inputs = inputs.reshape((sources * capacity,) + inputs.shape[2:])
    flat_pick = jnp.repeat(expert_pick, capacity)
    flat_flag = item_filled.reshape(-1)
    out_shape = (inputs.shape[2] - 2,) + inputs.shape[3:]

    def single(item):
        window, pick_one, flag_item = item
        return lax.cond(
            flag_item,
            lambda: convolve(window, kernels[pick_one]).astype(jnp.bfloat16),
            lambda: jnp.zeros(out_shape, jnp.bfloat16),
        )

    computed = lax.map(single, (flat_inputs, flat_pick, flat_flag))
    return computed.reshape((sources, capacity) + out_shape)


def owner_transpose(grad_items, expert_pick, item_filled, kernels):
    sources, capacity = (grad_items.shape[0], grad_items.shape[1])
    flat_grads = grad_items.reshape((sources * capacity,) + grad_items.shape[2:])
    flat_pick = jnp.repeat(expert_pick, capacity)
    flat_flag = item_filled.reshape(-1)
    out_shape = (grad_items.shape[2] + 2, grad_items.shape[3], kernels.shape[2])

    def single(item):
        grad_one, pick_one, flag_item = item
        return lax.cond(
            flag_item,
            lambda: transpose_conv(grad_one, kernels[pick_one]).astype(jnp.bfloat16),
            lambda: jnp.zeros(out_shape, jnp.bfloat16),
        )

    computed = lax.map(single, (flat_grads, flat_pick, flat_flag))
    return computed.reshape((sources, capacity) + out_shape)


def owner_kernel_terms(inputs, grad_items, expert_pick, local_count):
    sources, capacity = (inputs.shape[0], inputs.shape[1])
    number_of_rows = grad_items.shape[2]
    columns = grad_items.shape[3]
    channels = inputs.shape[4]
    widened = jnp.pad(inputs, ((0, 0), (0, 0), (0, 0), (1, 1), (0, 0)))
    flat_grad = grad_items.reshape(sources, capacity * number_of_rows * columns, channels)
    pieces = []
    for row_off in range(3):
        for col_off in range(3):
            patch = widened[
                :, :, row_off : row_off + number_of_rows, col_off : col_off + columns
            ].reshape(sources, capacity * number_of_rows * columns, channels)
            pieces.append(
                lax.dot_general(
                    patch,
                    flat_grad,
                    (((1,), (1,)), ((0,), (0,))),
                    preferred_element_type=jnp.float32,
                )
            )
    tap_terms = jnp.stack(pieces, axis=1)
    onehot = (expert_pick[:, None] == jnp.arange(local_count)[None, :]).astype(jnp.float32)
    return jnp.einsum("oe,otij->etij", onehot, tap_terms, precision=highest)


def shards(frames, kernels, experts, counts, gate_weights, cotangent):
    owners_count = lax.axis_size("dp")
    specialist_within_tile = kernels.shape[0]
    capacity = CAP
    with_rim = padded(frames, (("tile", 1),), 1)
    center = frames.astype(jnp.float32)
    upstream = cotangent.astype(jnp.float32)
    chosen = experts[:, 0]
    number_of_frames, slot_count = chosen.shape
    active = jnp.arange(slot_count)[None, :] < counts[:, 0][:, None]
    gate_rows = gate_weights[:, 0]
    owner_of = chosen // specialist_within_tile
    local_of = chosen % specialist_within_tile
    named_owner = owner_of[:, :, None] == jnp.arange(owners_count)[None, None, :]
    slot_hit = named_owner & active[:, :, None]
    hit_float = slot_hit.astype(jnp.float32)
    wanted = jnp.any(slot_hit, axis=1)
    position = jnp.cumsum(wanted.astype(jnp.int32), axis=0) - 1
    slot_map = wanted.T[:, None, :] & (
        position.T[:, None, :] == jnp.arange(capacity)[None, :, None]
    )
    slot_float = slot_map.astype(jnp.float32)
    filled = jnp.any(slot_map, axis=2)
    local_request = jnp.max(jnp.where(slot_hit, local_of[:, :, None], -1), axis=(0, 1))
    request = jnp.concatenate([local_request[:, None], filled.astype(jnp.int32)], axis=1)
    asked = lax.all_to_all(request, "dp", split_axis=0, concat_axis=0, tiled=True)
    expert_pick = jnp.maximum(asked[:, 0], 0)
    item_filled = asked[:, 1:] > 0
    tile_gate = jnp.einsum("fso,fs->fo", hit_float, gate_rows, precision=highest)
    weight = jnp.einsum("ocf,fo->oc", slot_float, tile_gate, precision=highest)
    outgoing = jnp.einsum(
        "ocf,frwk->ocrwk",
        slot_map.astype(jnp.bfloat16),
        with_rim,
        preferred_element_type=jnp.float32,
    ).astype(jnp.bfloat16)
    inputs = lax.all_to_all(outgoing, "dp", split_axis=0, concat_axis=0, tiled=True)
    computed = owner_forward(inputs, expert_pick, item_filled, kernels)
    returned = lax.all_to_all(computed, "dp", split_axis=0, concat_axis=0, tiled=True)
    activated, slope = activation(returned.astype(jnp.float32))
    combined = weight[:, :, None, None, None] * activated
    result = center + jnp.einsum("ocf,ocrwk->frwk", slot_float, combined, precision=highest)
    per_item = jnp.einsum("frwk,ocrwk->ocf", upstream, activated, precision=highest)
    selected_entries = jnp.sum(slot_float * per_item, axis=1)
    gate_grad = jnp.einsum("fso,of->fs", hit_float, selected_entries, precision=highest)
    upstream_item = jnp.einsum("ocf,frwk->ocrwk", slot_float, upstream, precision=highest)
    grad_pre = (upstream_item * weight[:, :, None, None, None] * slope).astype(jnp.bfloat16)
    received = lax.all_to_all(grad_pre, "dp", split_axis=0, concat_axis=0, tiled=True)
    back_items = owner_transpose(received, expert_pick, item_filled, kernels)
    kernel_grad = owner_kernel_terms(inputs, received, expert_pick, specialist_within_tile)
    arrived = lax.all_to_all(back_items, "dp", split_axis=0, concat_axis=0, tiled=True)
    rim_sum = jnp.einsum(
        "ocf,ocrwk->frwk", slot_float, arrived.astype(jnp.float32), precision=highest
    )
    edge_rows = jnp.stack([rim_sum[:, 0], rim_sum[:, -1]], axis=1)
    outer_rows = padded(edge_rows.astype(jnp.bfloat16), (("tile", 1),), 1).astype(edge_rows.dtype)
    inner_rows = rim_sum[:, 1:-1]
    inner_rows = inner_rows.at[:, 0].add(outer_rows[:, 0])
    inner_rows = inner_rows.at[:, -1].add(outer_rows[:, 3])
    input_grad = (upstream + inner_rows).astype(jnp.bfloat16)
    kernel_part = lax.psum_scatter(kernel_grad, "tile", scatter_dimension=3, tiled=True)
    return (result.astype(jnp.bfloat16), input_grad, gate_grad[:, None, :], kernel_part)


def solution(mesh):
    return jax.shard_map(
        shards,
        mesh=mesh,
        in_specs=(
            P("dp", "tile", None, None),
            P("dp", None, None, None),
            P("dp", "tile", None),
            P("dp", "tile"),
            P("dp", "tile", None),
            P("dp", "tile", None, None),
        ),
        out_specs=(
            P("dp", "tile", None, None),
            P("dp", "tile", None, None),
            P("dp", "tile", None),
            P("dp", None, None, "tile"),
        ),
        check_vma=False,
    )
```

profile of v0, /device:TPU:0, one launch (start us, length us, event | category | flops | bytes accessed | tf_op | source)
XLA Modules:
  0.0 620.9 jit_solution(17338980695180665500)
XLA Ops:
  32.4 36.8 %all-to-all-done.1 = bf16[8,2,3,64,256]{4,3,2,1,0:T(8,128)(2,1)S(1)} async-done(((bf16[8,2,3,64,256]{4,3,2,1,0:T(8,128)(2,1)}), bf16[8,2,3,64,256]{4,3,2,1,0:T(8,128)(2,1)S(1)}, u32[]{:S(2)}, u32[]{:S(2)}) %all-to-all-start.1) | async-done | bytes 1572896 | tf_op jit(solution)/shard_map/all_to_all | solution.py:165
  69.2 189.4 %while.24 = (s32[]{:T(128)}, bf16[16,1,64,256]{3,2,1,0:T(8,128)(2,1)}, pred[16]{0:T(512)(128)(4,1)S(1)}, bf16[16,3,64,256]{3,2,1,0:T(8,128)(2,1)S(1)}, bf16[4,9,...) while((s32[]{:T(128)}, bf16[16,1,64,256]{3,2,1,0:T(8,128)(2,1)}, ...), condition=%wide.region_7.8_spmd.clone, body=%wide.region_4.7_spmd.clone.sunk | while | flops 75644928 | bytes 3213894 | solution.py:80
  84.6 12.3 %conditional.6 = (bf16[1,1,64,256]{3,2,1,0:T(8,128)(2,1)S(1)}) conditional(s32[]{:T(128)} %bitcast.267, () %tuple.110, (bf16[16,3,64,256]{3,2,1,0:T(8,128)(2,1)S(1)}, s32[]{:T(128)}, s32[8]{0:T(128)S(1)}, bf16[4,9,256,256]{3,2,1,0:T(8,128)(2,1)}) %tuple.111), branch_computations={%region_5.5_spmd, %region_6.6_spmd} | conditional | flops 75644928 | bytes 3147718 | solution.py:74
  98.7 12.3 %conditional.6 = (bf16[1,1,64,256]{3,2,1,0:T(8,128)(2,1)S(1)}) conditional(s32[]{:T(128)} %bitcast.267, () %tuple.110, (bf16[16,3,64,256]{3,2,1,0:T(8,128)(2,1)S(1)}, s32[]{:T(128)}, s32[8]{0:T(128)S(1)}, bf16[4,9,256,256]{3,2,1,0:T(8,128)(2,1)}) %tuple.111), branch_computations={%region_5.5_spmd, %region_6.6_spmd} | conditional | flops 75644928 | bytes 3147718 | solution.py:74
  112.9 12.3 %conditional.6 = (bf16[1,1,64,256]{3,2,1,0:T(8,128)(2,1)S(1)}) conditional(s32[]{:T(128)} %bitcast.267, () %tuple.110, (bf16[16,3,64,256]{3,2,1,0:T(8,128)(2,1)S(1)}, s32[]{:T(128)}, s32[8]{0:T(128)S(1)}, bf16[4,9,256,256]{3,2,1,0:T(8,128)(2,1)}) %tuple.111), branch_computations={%region_5.5_spmd, %region_6.6_spmd} | conditional | flops 75644928 | bytes 3147718 | solution.py:74
  143.0 12.3 %conditional.6 = (bf16[1,1,64,256]{3,2,1,0:T(8,128)(2,1)S(1)}) conditional(s32[]{:T(128)} %bitcast.267, () %tuple.110, (bf16[16,3,64,256]{3,2,1,0:T(8,128)(2,1)S(1)}, s32[]{:T(128)}, s32[8]{0:T(128)S(1)}, bf16[4,9,256,256]{3,2,1,0:T(8,128)(2,1)}) %tuple.111), branch_computations={%region_5.5_spmd, %region_6.6_spmd} | conditional | flops 75644928 | bytes 3147718 | solution.py:74
  306.9 19.0 %copy.209 = f32[8,9,256,256]{2,0,1,3:T(8,128)} copy(f32[8,9,256,256]{3,2,0,1:T(8,128)} %bitcast_dynamic-update-slice_fusion) | data formatting | bytes 37748736 | tf_op jit(solution)/shard_map/stack | solution.py:124
  325.9 15.0 %fusion.85 = f32[4,9,256,256]{2,0,1,3:T(4,128)} fusion(f32[8,9,256,256]{2,0,1,3:T(8,128)} %copy.209, s32[8]{0:T(128)S(1)} %get-tuple-element.442), kind=kOutput, calls=%fused_computation.172 | convolution fusion | flops 226492448 | bytes 28311584 | tf_op jit(solution)/shard_map/oe,otij->etij/dot_general | solution.py:126
  342.3 189.2 %while.25 = (s32[]{:T(128)}, bf16[16,3,64,256]{3,2,1,0:T(8,128)(2,1)S(1)}, pred[16]{0:T(512)(128)(4,1)S(1)}, bf16[16,1,64,256]{3,2,1,0:T(8,128)(2,1)S(1)}, bf16[...) while((s32[]{:T(128)}, bf16[16,3,64,256]{3,2,1,0:T(8,128)(2,1)S(1)}, ...), condition=%wide.region_11.12_spmd.clone, body=%wide.region_8.11_spmd.clone.sunk | while | flops 226934784 | bytes 6488642 | solution.py:99
  343.5 13.0 %conditional.7 = (bf16[1,3,64,256]{3,2,1,0:T(8,128)(2,1)S(1)}) conditional(s32[]{:T(128)} %bitcast.268, () %tuple.113, (bf16[16,1,64,256]{3,2,1,0:T(8,128)(2,1)S(1)}, s32[]{:T(128)}, s32[8]{0:T(128)S(1)}, bf16[4,9,256,256]{3,2,1,0:T(8,128)(2,1)}) %tuple.114), branch_computations={%region_9.9_spmd, %region_10.10_spmd} | conditional | flops 226934784 | bytes 6291902 | solution.py:93
  357.8 13.0 %conditional.7 = (bf16[1,3,64,256]{3,2,1,0:T(8,128)(2,1)S(1)}) conditional(s32[]{:T(128)} %bitcast.268, () %tuple.113, (bf16[16,1,64,256]{3,2,1,0:T(8,128)(2,1)S(1)}, s32[]{:T(128)}, s32[8]{0:T(128)S(1)}, bf16[4,9,256,256]{3,2,1,0:T(8,128)(2,1)}) %tuple.114), branch_computations={%region_9.9_spmd, %region_10.10_spmd} | conditional | flops 226934784 | bytes 6291902 | solution.py:93
  372.0 13.0 %conditional.7 = (bf16[1,3,64,256]{3,2,1,0:T(8,128)(2,1)S(1)}) conditional(s32[]{:T(128)} %bitcast.268, () %tuple.113, (bf16[16,1,64,256]{3,2,1,0:T(8,128)(2,1)S(1)}, s32[]{:T(128)}, s32[8]{0:T(128)S(1)}, bf16[4,9,256,256]{3,2,1,0:T(8,128)(2,1)}) %tuple.114), branch_computations={%region_9.9_spmd, %region_10.10_spmd} | conditional | flops 226934784 | bytes 6291902 | solution.py:93
  386.3 13.0 %conditional.7 = (bf16[1,3,64,256]{3,2,1,0:T(8,128)(2,1)S(1)}) conditional(s32[]{:T(128)} %bitcast.268, () %tuple.113, (bf16[16,1,64,256]{3,2,1,0:T(8,128)(2,1)S(1)}, s32[]{:T(128)}, s32[8]{0:T(128)S(1)}, bf16[4,9,256,256]{3,2,1,0:T(8,128)(2,1)}) %tuple.114), branch_computations={%region_9.9_spmd, %region_10.10_spmd} | conditional | flops 226934784 | bytes 6291902 | solution.py:93
  400.5 13.0 %conditional.7 = (bf16[1,3,64,256]{3,2,1,0:T(8,128)(2,1)S(1)}) conditional(s32[]{:T(128)} %bitcast.268, () %tuple.113, (bf16[16,1,64,256]{3,2,1,0:T(8,128)(2,1)S(1)}, s32[]{:T(128)}, s32[8]{0:T(128)S(1)}, bf16[4,9,256,256]{3,2,1,0:T(8,128)(2,1)}) %tuple.114), branch_computations={%region_9.9_spmd, %region_10.10_spmd} | conditional | flops 226934784 | bytes 6291902 | solution.py:93
  416.1 13.0 %conditional.7 = (bf16[1,3,64,256]{3,2,1,0:T(8,128)(2,1)S(1)}) conditional(s32[]{:T(128)} %bitcast.268, () %tuple.113, (bf16[16,1,64,256]{3,2,1,0:T(8,128)(2,1)S(1)}, s32[]{:T(128)}, s32[8]{0:T(128)S(1)}, bf16[4,9,256,256]{3,2,1,0:T(8,128)(2,1)}) %tuple.114), branch_computations={%region_9.9_spmd, %region_10.10_spmd} | conditional | flops 226934784 | bytes 6291902 | solution.py:93
  431.7 13.0 %conditional.7 = (bf16[1,3,64,256]{3,2,1,0:T(8,128)(2,1)S(1)}) conditional(s32[]{:T(128)} %bitcast.268, () %tuple.113, (bf16[16,1,64,256]{3,2,1,0:T(8,128)(2,1)S(1)}, s32[]{:T(128)}, s32[8]{0:T(128)S(1)}, bf16[4,9,256,256]{3,2,1,0:T(8,128)(2,1)}) %tuple.114), branch_computations={%region_9.9_spmd, %region_10.10_spmd} | conditional | flops 226934784 | bytes 6291902 | solution.py:93
  445.9 13.0 %conditional.7 = (bf16[1,3,64,256]{3,2,1,0:T(8,128)(2,1)S(1)}) conditional(s32[]{:T(128)} %bitcast.268, () %tuple.113, (bf16[16,1,64,256]{3,2,1,0:T(8,128)(2,1)S(1)}, s32[]{:T(128)}, s32[8]{0:T(128)S(1)}, bf16[4,9,256,256]{3,2,1,0:T(8,128)(2,1)}) %tuple.114), branch_computations={%region_9.9_spmd, %region_10.10_spmd} | conditional | flops 226934784 | bytes 6291902 | solution.py:93
  460.2 13.0 %conditional.7 = (bf16[1,3,64,256]{3,2,1,0:T(8,128)(2,1)S(1)}) conditional(s32[]{:T(128)} %bitcast.268, () %tuple.113, (bf16[16,1,64,256]{3,2,1,0:T(8,128)(2,1)S(1)}, s32[]{:T(128)}, s32[8]{0:T(128)S(1)}, bf16[4,9,256,256]{3,2,1,0:T(8,128)(2,1)}) %tuple.114), branch_computations={%region_9.9_spmd, %region_10.10_spmd} | conditional | flops 226934784 | bytes 6291902 | solution.py:93
  474.4 13.0 %conditional.7 = (bf16[1,3,64,256]{3,2,1,0:T(8,128)(2,1)S(1)}) conditional(s32[]{:T(128)} %bitcast.268, () %tuple.113, (bf16[16,1,64,256]{3,2,1,0:T(8,128)(2,1)S(1)}, s32[]{:T(128)}, s32[8]{0:T(128)S(1)}, bf16[4,9,256,256]{3,2,1,0:T(8,128)(2,1)}) %tuple.114), branch_computations={%region_9.9_spmd, %region_10.10_spmd} | conditional | flops 226934784 | bytes 6291902 | solution.py:93
  488.7 13.0 %conditional.7 = (bf16[1,3,64,256]{3,2,1,0:T(8,128)(2,1)S(1)}) conditional(s32[]{:T(128)} %bitcast.268, () %tuple.113, (bf16[16,1,64,256]{3,2,1,0:T(8,128)(2,1)S(1)}, s32[]{:T(128)}, s32[8]{0:T(128)S(1)}, bf16[4,9,256,256]{3,2,1,0:T(8,128)(2,1)}) %tuple.114), branch_computations={%region_9.9_spmd, %region_10.10_spmd} | conditional | flops 226934784 | bytes 6291902 | solution.py:93
  504.3 13.0 %conditional.7 = (bf16[1,3,64,256]{3,2,1,0:T(8,128)(2,1)S(1)}) conditional(s32[]{:T(128)} %bitcast.268, () %tuple.113, (bf16[16,1,64,256]{3,2,1,0:T(8,128)(2,1)S(1)}, s32[]{:T(128)}, s32[8]{0:T(128)S(1)}, bf16[4,9,256,256]{3,2,1,0:T(8,128)(2,1)}) %tuple.114), branch_computations={%region_9.9_spmd, %region_10.10_spmd} | conditional | flops 226934784 | bytes 6291902 | solution.py:93
  518.5 12.9 %conditional.7 = (bf16[1,3,64,256]{3,2,1,0:T(8,128)(2,1)S(1)}) conditional(s32[]{:T(128)} %bitcast.268, () %tuple.113, (bf16[16,1,64,256]{3,2,1,0:T(8,128)(2,1)S(1)}, s32[]{:T(128)}, s32[8]{0:T(128)S(1)}, bf16[4,9,256,256]{3,2,1,0:T(8,128)(2,1)}) %tuple.114), branch_computations={%region_9.9_spmd, %region_10.10_spmd} | conditional | flops 226934784 | bytes 6291902 | solution.py:93
  545.8 14.3 %all-to-all-done.4 = bf16[8,2,3,64,256]{4,1,3,2,0:T(2,128)(2,1)S(1)} async-done(((bf16[8,2,3,64,256]{4,1,3,2,0:T(2,128)(2,1)}), bf16[8,2,3,64,256]{4,1,3,2,0:T(2,128)(2,1)S(1)}, u32[]{:S(2)}, u32[]{:S(2)}) %all-to-all-start.4) | async-done | bytes 1572896 | tf_op jit(solution)/shard_map/all_to_all | solution.py:179
  562.5 45.7 %collective-permute-start.2 = (bf16[4,1,64,256]{3,0,2,1:T(4,128)(2,1)S(1)}, bf16[4,1,64,256]{3,0,2,1:T(4,128)(2,1)S(1)}, u32[]{:S(2)}, u32[]{:S(2)}) collective-permute-start(bf16[4,1,64,256]{3,0,2,1:T(4,128)(2,1)S(1)} %get-tuple-element.300), channel_id=1, source_target_pairs={{0,1},{1,2},{2,3},{4,5},{5,6},{6,7},{8,9},{9,10},{10,11},{12,13},{... | collective-permute-start | bytes 393224 | tf_op jit(solution)/shard_map/ppermute | solution.py:19
  (527 shorter events, 512.3 us)
Async XLA Ops:
  7.2 255.1 %copy-start = (f32[4,1,4]{2,1,0:T(1,128)S(1)}, f32[4,1,4]{2,1,0:T(1,128)}, u32[]{:S(2)}) copy-start(f32[4,1,4]{2,1,0:T(1,128)} %param.22) | copy-start | bytes 196
  8.2 13.9 %collective-permute-start.1 = (bf16[4,1,64,256]{3,0,2,1:T(4,128)(2,1)S(1)}, bf16[4,1,64,256]{3,0,2,1:T(4,128)(2,1)S(1)}, u32[]{:S(2)}, u32[]{:S(2)}) collective-permute-start(bf16[4,1,64,256]{3,0,2,1:T(4,128)(2,1)S(1)} %copy.147), channel_id=1, source_target_pairs={{1,0},{2,1},{3,2},{5,4},{6,5},{7,6},{9,8},{10,9},{11,10},{13,12},{... | collective-permute-start | bytes 393224 | tf_op jit(solution)/shard_map/ppermute | solution.py:20
  9.5 12.7 %collective-permute-start = (bf16[4,1,64,256]{3,0,2,1:T(4,128)(2,1)S(1)}, bf16[4,1,64,256]{3,0,2,1:T(4,128)(2,1)S(1)}, u32[]{:S(2)}, u32[]{:S(2)}) collective-permute-start(bf16[4,1,64,256]{3,0,2,1:T(4,128)(2,1)S(1)} %copy.147), channel_id=1, source_target_pairs={{0,1},{1,2},{2,3},{4,5},{5,6},{6,7},{8,9},{9,10},{10,11},{12,13},{... | collective-permute-start | bytes 393224 | tf_op jit(solution)/shard_map/ppermute | solution.py:19
  14.9 13.7 %all-to-all-start = ((s32[8,1,3]{2,1,0:T(1,128)}), s32[8,1,3]{2,1,0:T(1,128)S(1)}, u32[]{:S(2)}, u32[]{:S(2)}) async-start(s32[8,1,3]{2,1,0:T(1,128)} %copy.148), calls=%async_computation | async-start | bytes 8192 | tf_op jit(solution)/shard_map/all_to_all | solution.py:154
  28.6 40.7 %all-to-all-start.1 = ((bf16[8,2,3,64,256]{4,3,2,1,0:T(8,128)(2,1)}), bf16[8,2,3,64,256]{4,3,2,1,0:T(8,128)(2,1)S(1)}, u32[]{:S(2)}, u32[]{:S(2)}) async-start(bf16[8,2,3,64,256]{4,3,2,1,0:T(8,128)(2,1)} %copy.154), calls=%async_computation.1 | async-start | bytes 3145728 | tf_op jit(solution)/shard_map/all_to_all | solution.py:165
  69.2 203.3 %copy-start.11 = (bf16[4,1,64,256]{3,2,1,0:T(8,128)(2,1)S(1)}, bf16[4,1,64,256]{3,2,1,0:T(8,128)(2,1)}, u32[]{:S(2)}) copy-start(bf16[4,1,64,256]{3,2,1,0:T(8,128)(2,1)} %param.23) | copy-start | bytes 393220
  258.6 13.9 %all-to-all-start.2 = ((bf16[8,2,1,64,256]{4,3,1,2,0:T(8,128)(2,1)}), bf16[8,2,1,64,256]{4,3,1,2,0:T(8,128)(2,1)S(1)}, u32[]{:S(2)}, u32[]{:S(2)}) async-start(bf16[8,2,1,64,256]{4,3,1,2,0:T(8,128)(2,1)} %bitcast.64), calls=%async_computation.2 | async-start | bytes 1048576 | tf_op jit(solution)/shard_map/all_to_all | solution.py:167
  272.5 1.7 copy-start.8
  274.2 14.1 %all-to-all-start.3 = ((bf16[8,2,1,64,256]{4,3,1,2,0:T(8,128)(2,1)}), bf16[8,2,1,64,256]{4,3,1,2,0:T(8,128)(2,1)S(1)}, u32[]{:S(2)}, u32[]{:S(2)}) async-start(bf16[8,2,1,64,256]{4,3,1,2,0:T(8,128)(2,1)} %copy.160), calls=%async_computation.3 | async-start | bytes 1048576 | tf_op jit(solution)/shard_map/all_to_all | solution.py:176
  277.9 332.2 %all-reduce.6.cloned.1.call-start = ((), (), s32[]{:S(2)}) async-start(), calls=%async_computation.5 | async-start | bytes 18874368
  280.9 13.2 %copy-start.6 = (bf16[8,2,1,64,256]{4,3,1,0,2:T(8,128)(2,1)S(1)}, bf16[8,2,1,64,256]{4,3,1,0,2:T(8,128)(2,1)}, u32[]{:S(2)}) copy-start(bf16[8,2,1,64,256]{4,3,1,0,2:T(8,128)(2,1)} %get-tuple-element.292) | copy-start | bytes 1572868
  288.3 7.6 %copy-start.5 = (bf16[8,2,1,64,256]{4,3,1,0,2:T(8,128)(2,1)S(1)}, bf16[8,2,1,64,256]{4,3,1,0,2:T(8,128)(2,1)}, u32[]{:S(2)}) copy-start(bf16[8,2,1,64,256]{4,3,1,0,2:T(8,128)(2,1)} %get-tuple-element.293) | copy-start | bytes 1572868
  291.2 6.6 %copy-start.4 = (bf16[8,2,1,64,256]{4,3,1,0,2:T(8,128)(2,1)S(1)}, bf16[8,2,1,64,256]{4,3,1,0,2:T(8,128)(2,1)}, u32[]{:S(2)}) copy-start(bf16[8,2,1,64,256]{4,3,1,0,2:T(8,128)(2,1)} %get-tuple-element.297) | copy-start | bytes 1572868
  294.1 5.6 copy-start.3
  295.9 5.6 copy-start.2
  340.9 1.4 copy-start.7
  531.5 6.8 %copy-start.12 = (u32[32]{0:T(128)S(1)}, u32[32]{0:T(128)}, u32[]{:S(2)}) copy-start(u32[32]{0:T(128)} %constant.160) | copy-start | bytes 388
  531.5 8.0 %copy-start.10 = (bf16[4,1,64,256]{3,2,1,0:T(8,128)(2,1)S(1)}, bf16[4,1,64,256]{3,2,1,0:T(8,128)(2,1)}, u32[]{:S(2)}) copy-start(bf16[4,1,64,256]{3,2,1,0:T(8,128)(2,1)} %param.18) | copy-start | bytes 393220
  534.3 7.9 %copy-start.9 = (bf16[8,2,1,64,256]{4,3,1,2,0:T(8,128)(2,1)S(1)}, bf16[8,2,1,64,256]{4,3,1,2,0:T(8,128)(2,1)}, u32[]{:S(2)}) copy-start(bf16[8,2,1,64,256]{4,3,1,2,0:T(8,128)(2,1)} %copy-done.8) | copy-start | bytes 1572868
  534.3 25.8 %all-to-all-start.4 = ((bf16[8,2,3,64,256]{4,1,3,2,0:T(2,128)(2,1)}), bf16[8,2,3,64,256]{4,1,3,2,0:T(2,128)(2,1)S(1)}, u32[]{:S(2)}, u32[]{:S(2)}) async-start(bf16[8,2,3,64,256]{4,1,3,2,0:T(2,128)(2,1)} %copy.162), calls=%async_computation.4 | async-start | bytes 3145728 | tf_op jit(solution)/shard_map/all_to_all | solution.py:179
  561.2 47.7 %collective-permute-start.3 = (bf16[4,1,64,256]{3,0,2,1:T(4,128)(2,1)S(1)}, bf16[4,1,64,256]{3,0,2,1:T(4,128)(2,1)S(1)}, u32[]{:S(2)}, u32[]{:S(2)}) collective-permute-start(bf16[4,1,64,256]{3,0,2,1:T(4,128)(2,1)S(1)} %get-tuple-element.301), channel_id=1, source_target_pairs={{1,0},{2,1},{3,2},{5,4},{6,5},{7,6},{9,8},{10,9},{11,10},{13,12},{... | collective-permute-start | bytes 393224 | tf_op jit(solution)/shard_map/ppermute | solution.py:20
  562.5 46.7 %collective-permute-start.2 = (bf16[4,1,64,256]{3,0,2,1:T(4,128)(2,1)S(1)}, bf16[4,1,64,256]{3,0,2,1:T(4,128)(2,1)S(1)}, u32[]{:S(2)}, u32[]{:S(2)}) collective-permute-start(bf16[4,1,64,256]{3,0,2,1:T(4,128)(2,1)S(1)} %get-tuple-element.300), channel_id=1, source_target_pairs={{0,1},{1,2},{2,3},{4,5},{5,6},{6,7},{8,9},{9,10},{10,11},{12,13},{... | collective-permute-start | bytes 393224 | tf_op jit(solution)/shard_map/ppermute | solution.py:19
  609.4 4.6 copy-start.1
Sparse Core Ops, SparseCore 0:
  341.0 187.3 all-reduce.5
where the time goes:
time: 629 us; the launch traced here: 621 us
  matrix products  298 us (47%)
  local copies, waits for them, and re-layouts  86.2 us (14%)
  loops' own time  73.5 us (12%)
  starting transfers between devices  73.4 us (12%)
  waiting for transfers between devices  73.1 us (12%)
  between operations  14.9 us (2%)
    dot_general x117, matrix products, transpose_conv(): lax.dot_general(patch, kernel_weight[3 * row_off + col_off], (((1,), (1,)...  131 us
    dot_general x117, matrix products, convolve(): jnp.dot(patch, kernel_weight[3 * row_off + col_off], preferred_element_ty...  124 us
    ppermute x2, starting transfers between devices, padded(): before = lax.ppermute(last, axis, up)  48.7 us
    all_to_all x1, waiting for transfers between devices, shards(): lax.all_to_all(outgoing, 'dp', split_axis=0, concat_axis=0, tiled=True)  36.8 us
    dynamic_slice x58, local copies, waits for them, and re-layouts, owner_forward(): computed = lax.map(single, (flat_inputs, flat_pick, flat_flag))  34.1 us
    another operation x16, loops' own time, single(): lax.cond(flag_item, lambda: transpose_conv(grad_one, kernels[pick_one]).a...  26.4 us
    another operation x16, loops' own time, single(): lax.cond(flag_item, lambda: convolve(window, kernels[pick_one]).astype(jn...  25.8 us
    another operation x1, local copies, waits for them, and re-layouts, owner_kernel_terms(): tap_terms = jnp.stack(pieces, axis=1)  19 us
  transfers between devices with their start and end apart: 10, of which 6 were waited for; matrix products, arithmetic and copies ran while one was open for 28% of the time, Pallas kernels for 0%

commit v1 on v0

v1 whole, which is shorter than its diff:
```python
import functools

import jax
import jax.numpy as jnp
from jax import lax
from jax.experimental import pallas as pl
from jax.experimental.pallas import tpu as pltpu
from jax.sharding import PartitionSpec as P

CAP = 2


def shifts(columns, rows):
    place = lax.broadcasted_iota(jnp.int32, (rows, 1), 0) % columns

    def later(v):
        return jnp.where(place == 0, 0.0, pltpu.roll(v, 1, 0))

    def sooner(v):
        return jnp.where(place == columns - 1, 0.0, pltpu.roll(v, rows - 1, 0))

    return later, sooner


def owner_kernel(pick_ref, weight_ref, items_ref, bank_ref, back_ref, gate_ref, grad_ref):
    s = pl.program_id(0)
    cap, _, columns, channels = items_ref.shape[1:]
    rows = cap * columns
    later, sooner = shifts(columns, rows)

    @pl.when(s == 0)
    def _():
        grad_ref[...] = jnp.zeros_like(grad_ref)

    item = lax.broadcasted_iota(jnp.int32, (rows, 1), 0) // columns
    weight = jnp.zeros((rows, 1), jnp.float32)
    for c in range(cap):
        weight = jnp.where(item == c, weight_ref[s, c], weight)

    window = [items_ref[0, :, r].reshape(rows, channels) for r in range(3)]
    upstream = items_ref[0, :, 3].reshape(rows, channels).astype(jnp.float32)

    def column_term(db):
        total = jnp.dot(window[0], bank_ref[0, db], preferred_element_type=jnp.float32)
        for da in (1, 2):
            total = total + jnp.dot(
                window[da], bank_ref[0, 3 * da + db], preferred_element_type=jnp.float32
            )
        return total

    pre = column_term(1) + later(column_term(0)) + sooner(column_term(2))
    pre = pre.astype(jnp.bfloat16).astype(jnp.float32)
    squash = jax.nn.sigmoid(pre)
    activated = pre * squash
    slope = squash * (1.0 + pre * (1.0 - squash))
    back_ref[0, :, 3] = (weight * activated).astype(jnp.bfloat16).reshape(cap, columns, channels)
    gates = jnp.sum((upstream * activated).reshape(cap, columns, channels), axis=1)
    gate_ref[0] = jnp.broadcast_to(jnp.sum(gates, axis=1, keepdims=True), gate_ref.shape[1:])

    grad = (upstream * weight * slope).astype(jnp.bfloat16)
    for da in range(3):
        parts = [
            lax.dot_general(
                grad,
                bank_ref[0, 3 * da + db],
                (((1,), (1,)), ((), ())),
                preferred_element_type=jnp.float32,
            )
            for db in range(3)
        ]
        total = parts[1] + sooner(parts[0]) + later(parts[2])
        back_ref[0, :, da] = total.astype(jnp.bfloat16).reshape(cap, columns, channels)

    grad_wide = grad.astype(jnp.float32)
    moved = [sooner(grad_wide).astype(jnp.bfloat16), grad, later(grad_wide).astype(jnp.bfloat16)]
    e = pick_ref[s]
    chunks, _, _, share, _ = grad_ref.shape
    for db in range(3):
        for da in range(3):
            term = lax.dot_general(
                moved[db], window[da], (((0,), (0,)), ((), ())), preferred_element_type=jnp.float32
            )
            grad_ref[:, e, 3 * da + db] += term.reshape(chunks, share, channels)


def owner(pick, weight, items, kernels, chunks):
    sources, cap, _, columns, channels = items.shape
    experts, taps, _, outputs = kernels.shape
    spec = pltpu.PrefetchScalarGridSpec(
        num_scalar_prefetch=2,
        grid=(sources,),
        in_specs=[
            pl.BlockSpec((1, cap, 4, columns, channels), lambda s, p, w: (s, 0, 0, 0, 0)),
            pl.BlockSpec((1, taps, channels, outputs), lambda s, p, w: (p[s], 0, 0, 0)),
        ],
        out_specs=[
            pl.BlockSpec((1, cap, 4, columns, channels), lambda s, p, w: (s, 0, 0, 0, 0)),
            pl.BlockSpec((1, cap, 128), lambda s, p, w: (s, 0, 0)),
            pl.BlockSpec(
                (chunks, experts, taps, outputs // chunks, channels),
                lambda s, p, w: (0, 0, 0, 0, 0),
                pipeline_mode=pl.Buffered(1),
            ),
        ],
    )
    return pl.pallas_call(
        owner_kernel,
        grid_spec=spec,
        out_shape=[
            jax.ShapeDtypeStruct((sources, cap, 4, columns, channels), jnp.bfloat16),
            jax.ShapeDtypeStruct((sources, cap, 128), jnp.float32),
            jax.ShapeDtypeStruct(
                (chunks, experts, taps, outputs // chunks, channels), jnp.float32
            ),
        ],
        compiler_params=pltpu.CompilerParams(vmem_limit_bytes=48 * 1024 * 1024),
        name="owner",
    )(pick, weight, items, kernels)


def swap(x):
    return lax.all_to_all(x, "dp", split_axis=0, concat_axis=0, tiled=True)


def line(count):
    up = [(i, i + 1) for i in range(count - 1)]
    return up, [(j, i) for i, j in up]


def shards(frames, kernels, experts, counts, gate_weights, cotangent):
    owners = lax.axis_size("dp")
    tiles = lax.axis_size("tile")
    local = kernels.shape[0]
    up, down = line(tiles)
    before = lax.ppermute(frames[:, -1:], "tile", up)
    after = lax.ppermute(frames[:, :1], "tile", down)
    sheet = jnp.concatenate([before, frames, after, cotangent], axis=1)

    chosen = experts[:, 0]
    frame_count, slots = chosen.shape
    active = jnp.arange(slots)[None, :] < counts[:, 0][:, None]
    owner_of = chosen // local
    hit = (owner_of[:, :, None] == jnp.arange(owners)) & active[:, :, None]
    wanted = jnp.any(hit, axis=1)
    position = jnp.cumsum(wanted.astype(jnp.int32), axis=0) - 1
    slot_map = wanted.T[:, None, :] & (
        position.T[:, None, :] == jnp.arange(CAP)[None, :, None]
    )
    request = jnp.max(jnp.where(hit, (chosen % local)[:, :, None], 0), axis=(0, 1))
    tile_gate = jnp.sum(jnp.where(hit, gate_weights[:, 0][:, :, None], 0.0), axis=1)
    weight = jnp.sum(jnp.where(slot_map, tile_gate.T[:, None, :], 0.0), axis=2)
    note = jnp.concatenate([request[:, None].astype(jnp.float32), weight], axis=1)
    noted = swap(note)
    pick = noted[:, 0].astype(jnp.int32)
    shares = noted[:, 1:]

    picked = slot_map.astype(jnp.bfloat16).reshape(owners * CAP, frame_count)
    outgoing = jnp.dot(
        picked, sheet.reshape(frame_count, -1), preferred_element_type=jnp.float32
    ).astype(jnp.bfloat16)
    items = swap(outgoing.reshape((owners, CAP) + sheet.shape[1:]))

    back, gates, bank_grad = owner(pick, shares, items, kernels, tiles)
    kernel_part = lax.psum_scatter(bank_grad, "tile", scatter_dimension=0, tiled=True)[0]
    kernel_part = jnp.swapaxes(kernel_part, 2, 3)

    arrived = swap(back)
    gates = swap(gates[:, :, 0])
    selected = jnp.sum(jnp.where(slot_map, gates[:, :, None], 0.0), axis=1)
    gate_grad = jnp.sum(jnp.where(hit, selected.T[:, None, :], 0.0), axis=2)

    gathered = jnp.dot(
        picked.T, arrived.reshape(owners * CAP, -1), preferred_element_type=jnp.float32
    ).reshape(sheet.shape)
    result = (frames.astype(jnp.float32) + gathered[:, 3:4]).astype(jnp.bfloat16)
    from_above = lax.ppermute(gathered[:, 2:3].astype(jnp.bfloat16), "tile", up)
    from_below = lax.ppermute(gathered[:, 0:1].astype(jnp.bfloat16), "tile", down)
    input_grad = (
        cotangent.astype(jnp.float32)
        + gathered[:, 1:2]
        + from_above.astype(jnp.float32)
        + from_below.astype(jnp.float32)
    ).astype(jnp.bfloat16)
    return (result, input_grad, gate_grad[:, None, :], kernel_part)


def solution(mesh):
    return jax.shard_map(
        shards,
        mesh=mesh,
        in_specs=(
            P("dp", "tile", None, None),
            P("dp", None, None, None),
            P("dp", "tile", None),
            P("dp", "tile"),
            P("dp", "tile", None),
            P("dp", "tile", None, None),
        ),
        out_specs=(
            P("dp", "tile", None, None),
            P("dp", "tile", None, None),
            P("dp", "tile", None),
            P("dp", None, None, "tile"),
        ),
        check_vma=False,
    )
```

time: 629 us -> 182 us (0.29); the launches traced: 621 us -> 181 us
  matrix products: 298 us -> 2.16 us
  local copies, waits for them, and re-layouts: 86.2 us -> 8.85 us
  loops' own time: 73.5 us -> 0 us
  starting transfers between devices: 73.4 us -> 24.6 us
  waiting for transfers between devices: 73.1 us -> 110 us
  Pallas kernels: 0 us -> 16 us
    dot_general x251 -> x2, matrix products: 298 us -> 2.16 us  [the longest x1 1.36 us: shards(): jnp.dot(picked.T, arrived.reshape(owners * CAP, -1), preferred_element_ty...]
    another operation x34 -> x0, loops' own time: 73.5 us -> none  [the longest x16 26.4 us: single(): lax.cond(flag_item, lambda: transpose_conv(grad_one, kernels[pick_one]).a...]
    ppermute x4, starting transfers between devices: 51.3 us -> 6.66 us  [the longest x1 2.41 us: shards(): before = lax.ppermute(frames[:, -1:], 'tile', up)]
    dynamic_slice x58 -> x0, local copies, waits for them, and re-layouts: 34.1 us -> none  [owner_forward(): computed = lax.map(single, (flat_inputs, flat_pick, flat_flag))]
    all_to_all x5 -> x4, waiting for transfers between devices: 72.8 us -> 99.4 us  [swap(): return lax.all_to_all(x, 'dp', split_axis=0, concat_axis=0, tiled=True)]
    another operation x1 -> x0, local copies, waits for them, and re-layouts: 19 us -> none  [owner_kernel_terms(): tap_terms = jnp.stack(pieces, axis=1)]
    pallas_call x0 -> x1, Pallas kernels: none -> 16 us  [owner(): pl.pallas_call(owner_kernel, grid_spec=spec, out_shape=[jax.ShapeDtypeStr...]
    dynamic_update_slice x32 -> x0, local copies, waits for them, and re-layouts: 10.2 us -> none  [the longest x16 9.99 us: owner_forward(): computed = lax.map(single, (flat_inputs, flat_pick, flat_flag))]
  transfers between devices with their start and end apart: 10 -> 9, of which waited for: 6 -> 5; matrix products, arithmetic and copies ran while one was open for 28% -> 9% of each run, Pallas kernels for 0% -> 0%
where the time goes in v1:
time: 182 us; the launch traced here: 181 us
  waiting for transfers between devices  110 us (60%)
  starting transfers between devices  24.6 us (14%)
  Pallas kernels  16 us (9%)
  between operations  14.2 us (8%)
  local copies, waits for them, and re-layouts  8.85 us (5%)
  other arithmetic  5.37 us (3%)
  matrix products  2.16 us (1%)
    all_to_all x4, waiting for transfers between devices, swap(): return lax.all_to_all(x, 'dp', split_axis=0, concat_axis=0, tiled=True)  99.4 us
    all_to_all x4, starting transfers between devices, swap(): return lax.all_to_all(x, 'dp', split_axis=0, concat_axis=0, tiled=True)  17.9 us
    pallas_call x1, Pallas kernels, owner(): pl.pallas_call(owner_kernel, grid_spec=spec, out_shape=[jax.ShapeDtypeStr...  16 us
    reduce_scatter x1, waiting for transfers between devices, shards(): lax.psum_scatter(bank_grad, 'tile', scatter_dimension=0, tiled=True)[0]  9.34 us
    unnamed x10, local copies, waits for them, and re-layouts  5.68 us
  transfers between devices with their start and end apart: 9, of which 5 were waited for; matrix products, arithmetic and copies ran while one was open for 9% of the time, Pallas kernels for 0%

profile of v1, /device:TPU:0, one launch (start us, length us, event | category | flops | bytes accessed | tf_op | source)
XLA Modules:
  0.0 181.5 jit_solution(7045368803906345132)
XLA Ops:
  7.2 2.4 %collective-permute-start = (bf16[4,1,64,256]{3,2,1,0:T(8,128)(2,1)}, bf16[4,1,64,256]{3,2,1,0:T(8,128)(2,1)S(1)}, u32[]{:S(2)}, u32[]{:S(2)}) collective-permute-start(bf16[4,1,64,256]{3,2,1,0:T(8,128)(2,1)} %param.6), channel_id=1, source_target_pairs={{0,1},{1,2},{2,3},{4,5},{5,6},{6,7},{8,9},{9,10},{10,11},{12,13},{... | collective-permute-start | bytes 393224 | tf_op jit(solution)/shard_map/ppermute | solution.py:135
  9.6 1.3 collective-permute-start.1
  10.9 0.7 add_select_fusion.1
  11.6 0.7 iota_compare_fusion.2
  12.5 0.8 select_reduce_fusion.3
  14.1 6.6 %all-to-all-start = ((f32[8,1,3]{2,1,0:T(1,128)}), f32[8,1,3]{2,1,0:T(1,128)S(1)}, u32[]{:S(2)}, u32[]{:S(2)}) async-start(f32[8,1,3]{2,1,0:T(1,128)} %bitcast.19), calls=%async_computation | async-start | bytes 8192 | tf_op jit(solution)/shard_map/all_to_all | solution.py:122
  20.9 1.0 pad_maximum_fusion
  22.4 0.8 convolution_convert_fusion
  23.2 1.8 copy.63
  24.9 2.2 %all-to-all-done = f32[8,1,3]{2,1,0:T(1,128)S(1)} async-done(((f32[8,1,3]{2,1,0:T(1,128)}), f32[8,1,3]{2,1,0:T(1,128)S(1)}, u32[]{:S(2)}, u32[]{:S(2)}) %all-to-all-start) | async-done | bytes 128 | tf_op jit(solution)/shard_map/all_to_all | solution.py:122
  27.1 3.8 %all-to-all-start.1 = ((bf16[8,2,4,64,256]{4,3,2,1,0:T(8,128)(2,1)}), bf16[8,2,4,64,256]{4,3,2,1,0:T(8,128)(2,1)S(1)}, u32[]{:S(2)}, u32[]{:S(2)}) async-start(bf16[8,2,4,64,256]{4,3,2,1,0:T(8,128)(2,1)} %bitcast.51), calls=%async_computation.1 | async-start | bytes 4194304 | tf_op jit(solution)/shard_map/all_to_all | solution.py:122
  31.2 49.2 %all-to-all-done.1.items_ref = bf16[8,2,4,64,256]{4,3,2,1,0:T(8,128)(2,1)S(1)} async-done(((bf16[8,2,4,64,256]{4,3,2,1,0:T(8,128)(2,1)}), bf16[8,2,4,64,256]{4,3,2,1,0:T(8,128)(2,1)S(1)}, u32[]{:S(2)}, u32[]{:S(2)}) %all-to-all-start.1) | async-done | bytes 2097184 | tf_op jit(solution)/shard_map/all_to_all | solution.py:122
  80.4 16.0 %owner.1 = (bf16[8,2,4,64,256]{4,3,2,1,0:T(8,128)(2,1)}, f32[8,2,128]{2,1,0:T(2,128)S(1)}, f32[4,4,9,64,256]{4,3,2,1,0:T(8,128)}) custom-call(s32[8]{0:T(128)S(1)} %convert_bitcast_fusion.pick_ref, f32[8,2]{1,0:T(8,128)S(1)} %copy.61.weight_ref, bf16[8,2,4,64,256]{4,3,2,1,0:T(8,128)(2,1)S(1)} %all-to-all-done.1.items_ref, bf16[4,9,256,256]{3,2,1,0:T(8,128)(2,1)} %bank_ref.1), custom_call_target="tpu_custom_call" | custom-call | tf_op jit(solution)/shard_map/owner/pallas_call | solution.py:106
  96.4 3.8 %all-to-all-start.2 = ((bf16[8,2,4,64,256]{4,3,2,1,0:T(8,128)(2,1)}), bf16[8,2,4,64,256]{4,3,2,1,0:T(8,128)(2,1)S(1)}, u32[]{:S(2)}, u32[]{:S(2)}) async-start(bf16[8,2,4,64,256]{4,3,2,1,0:T(8,128)(2,1)} %get-tuple-element.7), calls=%async_computation.2 | async-start | bytes 4194304 | tf_op jit(solution)/shard_map/all_to_all | solution.py:122
  100.4 0.7 copy.51
  101.1 48.0 %all-to-all-done.2 = bf16[8,2,4,64,256]{4,3,2,1,0:T(8,128)(2,1)S(1)} async-done(((bf16[8,2,4,64,256]{4,3,2,1,0:T(8,128)(2,1)}), bf16[8,2,4,64,256]{4,3,2,1,0:T(8,128)(2,1)S(1)}, u32[]{:S(2)}, u32[]{:S(2)}) %all-to-all-start.2) | async-done | bytes 2097184 | tf_op jit(solution)/shard_map/all_to_all | solution.py:122
  149.1 3.6 %all-to-all-start.3 = ((f32[8,1,2]{2,1,0:T(1,128)}), f32[8,1,2]{2,1,0:T(1,128)S(1)}, u32[]{:S(2)}, u32[]{:S(2)}) async-start(f32[8,1,2]{2,1,0:T(1,128)} %copy.51), calls=%async_computation.3 | async-start | bytes 8192 | tf_op jit(solution)/shard_map/all_to_all | solution.py:122
  152.7 2.0 %reshape.175 = bf16[16,65536]{1,0:T(8,128)(2,1)} reshape(bf16[8,2,4,64,256]{4,3,2,1,0:T(8,128)(2,1)S(1)} %all-to-all-done.2) | data formatting | bytes 4194304 | tf_op jit(solution)/shard_map/reshape | solution.py:173
  154.7 2.0 %copy.64 = bf16[2,8,256,256]{3,2,1,0:T(8,128)(2,1)S(1)} copy(bf16[2,8,256,256]{3,1,2,0:T(8,128)(2,1)} %bitcast.54) | data formatting | bytes 4194304
  156.7 1.4 fusion.12
  158.2 1.7 collective-permute-start.2
  159.9 1.3 collective-permute-start.3
  162.0 1.6 collective-permute-done.3
  165.3 9.3 %reduce-scatter.2.cloned.1.call-done = f32[1,4,9,64,256]{4,3,2,1,0:T(8,128)} async-done(((f32[4,4,9,64,256]{4,3,2,1,0:T(8,128)}), f32[1,4,9,64,256]{4,3,2,1,0:T(8,128)}) %reduce-scatter.2.cloned.1.call-update) | async-done | bytes 2359312 | tf_op jit(solution)/shard_map/reduce_scatter | solution.py:164
  (34 shorter events, 4.6 us)
Async XLA Ops:
  7.2 13.7 %collective-permute-start = (bf16[4,1,64,256]{3,2,1,0:T(8,128)(2,1)}, bf16[4,1,64,256]{3,2,1,0:T(8,128)(2,1)S(1)}, u32[]{:S(2)}, u32[]{:S(2)}) collective-permute-start(bf16[4,1,64,256]{3,2,1,0:T(8,128)(2,1)} %param.6), channel_id=1, source_target_pairs={{0,1},{1,2},{2,3},{4,5},{5,6},{6,7},{8,9},{9,10},{10,11},{12,13},{... | collective-permute-start | bytes 393224 | tf_op jit(solution)/shard_map/ppermute | solution.py:135
  9.6 11.3 %collective-permute-start.1 = (bf16[4,1,64,256]{3,2,1,0:T(8,128)(2,1)}, bf16[4,1,64,256]{3,2,1,0:T(8,128)(2,1)S(1)}, u32[]{:S(2)}, u32[]{:S(2)}) collective-permute-start(bf16[4,1,64,256]{3,2,1,0:T(8,128)(2,1)} %param.6), channel_id=1, source_target_pairs={{1,0},{2,1},{3,2},{5,4},{6,5},{7,6},{9,8},{10,9},{11,10},{13,12},{... | collective-permute-start | bytes 393224 | tf_op jit(solution)/shard_map/ppermute | solution.py:136
  14.1 13.0 %all-to-all-start = ((f32[8,1,3]{2,1,0:T(1,128)}), f32[8,1,3]{2,1,0:T(1,128)S(1)}, u32[]{:S(2)}, u32[]{:S(2)}) async-start(f32[8,1,3]{2,1,0:T(1,128)} %bitcast.19), calls=%async_computation | async-start | bytes 8192 | tf_op jit(solution)/shard_map/all_to_all | solution.py:122
  27.1 53.2 %all-to-all-start.1 = ((bf16[8,2,4,64,256]{4,3,2,1,0:T(8,128)(2,1)}), bf16[8,2,4,64,256]{4,3,2,1,0:T(8,128)(2,1)S(1)}, u32[]{:S(2)}, u32[]{:S(2)}) async-start(bf16[8,2,4,64,256]{4,3,2,1,0:T(8,128)(2,1)} %bitcast.51), calls=%async_computation.1 | async-start | bytes 4194304 | tf_op jit(solution)/shard_map/all_to_all | solution.py:122
  30.9 143.7 %reduce-scatter.2.cloned.1.call-start = ((), (), s32[]{:S(2)}) async-start(), calls=%async_computation.5 | async-start | bytes 11796480 | tf_op jit(solution)/shard_map/reduce_scatter | solution.py:164
  96.4 52.6 %all-to-all-start.2 = ((bf16[8,2,4,64,256]{4,3,2,1,0:T(8,128)(2,1)}), bf16[8,2,4,64,256]{4,3,2,1,0:T(8,128)(2,1)S(1)}, u32[]{:S(2)}, u32[]{:S(2)}) async-start(bf16[8,2,4,64,256]{4,3,2,1,0:T(8,128)(2,1)} %get-tuple-element.7), calls=%async_computation.2 | async-start | bytes 4194304 | tf_op jit(solution)/shard_map/all_to_all | solution.py:122
  149.1 12.1 %all-to-all-start.3 = ((f32[8,1,2]{2,1,0:T(1,128)}), f32[8,1,2]{2,1,0:T(1,128)S(1)}, u32[]{:S(2)}, u32[]{:S(2)}) async-start(f32[8,1,2]{2,1,0:T(1,128)} %copy.51), calls=%async_computation.3 | async-start | bytes 8192 | tf_op jit(solution)/shard_map/all_to_all | solution.py:122
  156.7 6.9 %copy-start = (bf16[4,1,64,256]{3,2,1,0:T(8,128)(2,1)S(1)}, bf16[4,1,64,256]{3,2,1,0:T(8,128)(2,1)}, u32[]{:S(2)}) copy-start(bf16[4,1,64,256]{3,2,1,0:T(8,128)(2,1)} %param.11) | copy-start | bytes 393220
  156.7 6.9 %copy-start.1 = (bf16[4,1,64,256]{3,2,1,0:T(8,128)(2,1)S(1)}, bf16[4,1,64,256]{3,2,1,0:T(8,128)(2,1)}, u32[]{:S(2)}) copy-start(bf16[4,1,64,256]{3,2,1,0:T(8,128)(2,1)} %param.6) | copy-start | bytes 393220
  158.2 3.8 %collective-permute-start.2 = (bf16[4,1,64,256]{3,0,2,1:T(4,128)(2,1)S(1)}, bf16[4,1,64,256]{3,0,2,1:T(4,128)(2,1)S(1)}, u32[]{:S(2)}, u32[]{:S(2)}) collective-permute-start(bf16[4,1,64,256]{3,0,2,1:T(4,128)(2,1)S(1)} %get-tuple-element.30), channel_id=1, source_target_pairs={{0,1},{1,2},{2,3},{4,5},{5,6},{6,7},{8,9},{9,10},{10,11},{12,13},{... | collective-permute-start | bytes 393224 | tf_op jit(solution)/shard_map/ppermute | solution.py:176
  159.9 3.8 %collective-permute-start.3 = (bf16[4,1,64,256]{3,0,2,1:T(4,128)(2,1)S(1)}, bf16[4,1,64,256]{3,0,2,1:T(4,128)(2,1)S(1)}, u32[]{:S(2)}, u32[]{:S(2)}) collective-permute-start(bf16[4,1,64,256]{3,0,2,1:T(4,128)(2,1)S(1)} %get-tuple-element.31), channel_id=1, source_target_pairs={{1,0},{2,1},{3,2},{5,4},{6,5},{7,6},{9,8},{10,9},{11,10},{13,12},{... | collective-permute-start | bytes 393224 | tf_op jit(solution)/shard_map/ppermute | solution.py:177
Sparse Core Ops, SparseCore 0:
  96.6 78.0 reduce-scatter.1

commit v2 on v1

--- a/solution.py
+++ b/solution.py
@@ -22,9 +22,12 @@
     return later, sooner
 
 
-def owner_kernel(pick_ref, weight_ref, items_ref, bank_ref, back_ref, gate_ref, grad_ref):
+def owner_kernel(
+    pick_ref, weight_ref, place_ref, rim_ref,
+    rows_ref, above_ref, below_ref, bank_ref, back_ref, gate_ref, grad_ref,
+):
     s = pl.program_id(0)
-    cap, _, columns, channels = items_ref.shape[1:]
+    cap, _, columns, channels = back_ref.shape[1:]
     rows = cap * columns
     later, sooner = shifts(columns, rows)
 
@@ -37,8 +40,16 @@
     for c in range(cap):
         weight = jnp.where(item == c, weight_ref[s, c], weight)
 
-    window = [items_ref[0, :, r].reshape(rows, channels) for r in range(3)]
-    upstream = items_ref[0, :, 3].reshape(rows, channels).astype(jnp.float32)
+    def gather(ref, *lead):
+        return jnp.concatenate([ref[(0,) + lead + (place_ref[s, c],)] for c in range(cap)], axis=0)
+
+    blank = jnp.zeros((rows, channels), jnp.bfloat16)
+    window = [
+        jnp.where(rim_ref[0] > 0, gather(above_ref), blank),
+        gather(rows_ref, 0),
+        jnp.where(rim_ref[1] > 0, gather(below_ref), blank),
+    ]
+    upstream = gather(rows_ref, 1).astype(jnp.float32)
 
     def column_term(db):
         total = jnp.dot(window[0], bank_ref[0, db], preferred_element_type=jnp.float32)
@@ -83,22 +94,24 @@
             grad_ref[:, e, 3 * da + db] += term.reshape(chunks, share, channels)
 
 
-def owner(pick, weight, items, kernels, chunks):
-    sources, cap, _, columns, channels = items.shape
+def owner(pick, weight, place, rim, rows, above, below, kernels, chunks):
+    sources, _, frames, columns, channels = rows.shape
     experts, taps, _, outputs = kernels.shape
     spec = pltpu.PrefetchScalarGridSpec(
-        num_scalar_prefetch=2,
+        num_scalar_prefetch=4,
         grid=(sources,),
         in_specs=[
-            pl.BlockSpec((1, cap, 4, columns, channels), lambda s, p, w: (s, 0, 0, 0, 0)),
-            pl.BlockSpec((1, taps, channels, outputs), lambda s, p, w: (p[s], 0, 0, 0)),
+            pl.BlockSpec((1, 2, frames, columns, channels), lambda s, *_: (s, 0, 0, 0, 0)),
+            pl.BlockSpec((1, frames, columns, channels), lambda s, *_: (s, 0, 0, 0)),
+            pl.BlockSpec((1, frames, columns, channels), lambda s, *_: (s, 0, 0, 0)),
+            pl.BlockSpec((1, taps, channels, outputs), lambda s, p, *_: (p[s], 0, 0, 0)),
         ],
         out_specs=[
-            pl.BlockSpec((1, cap, 4, columns, channels), lambda s, p, w: (s, 0, 0, 0, 0)),
-            pl.BlockSpec((1, cap, 128), lambda s, p, w: (s, 0, 0)),
+            pl.BlockSpec((1, CAP, 4, columns, channels), lambda s, *_: (s, 0, 0, 0, 0)),
+            pl.BlockSpec((1, CAP, 128), lambda s, *_: (s, 0, 0)),
             pl.BlockSpec(
                 (chunks, experts, taps, outputs // chunks, channels),
-                lambda s, p, w: (0, 0, 0, 0, 0),
+                lambda s, *_: (0, 0, 0, 0, 0),
                 pipeline_mode=pl.Buffered(1),
             ),
         ],
@@ -107,15 +120,215 @@
         owner_kernel,
         grid_spec=spec,
         out_shape=[
-            jax.ShapeDtypeStruct((sources, cap, 4, columns, channels), jnp.bfloat16),
-            jax.ShapeDtypeStruct((sources, cap, 128), jnp.float32),
+            jax.ShapeDtypeStruct((sources, CAP, 4, columns, channels), jnp.bfloat16),
+            jax.ShapeDtypeStruct((sources, CAP, 128), jnp.float32),
             jax.ShapeDtypeStruct(
                 (chunks, experts, taps, outputs // chunks, channels), jnp.float32
             ),
         ],
         compiler_params=pltpu.CompilerParams(vmem_limit_bytes=48 * 1024 * 1024),
         name="owner",
-    )(pick, weight, items, kernels)
+    )(pick, weight, place, rim, rows, above, below, kernels)
+
+
+def grid_of(owners):
+    across = 1
+    while across * across * 4 <= owners:
+        across *= 2
+    while owners % across:
+        across -= 1
+    return owners // across, across
+
+
+def remote(src, dst, send, recv, dp, tile):
+    return pltpu.make_async_remote_copy(
+        src_ref=src,
+        dst_ref=dst,
+        send_sem=send,
+        recv_sem=recv,
+        device_id=(dp, tile),
+        device_id_type=pl.DeviceIdType.MESH,
+    )
+
+
+def spread_kernel(
+    deep, across, tiles,
+    own_ref, note_ref, rows_ref, above_ref, below_ref, noted_ref,
+    local_sem, main_recv, above_recv, below_recv, note_recv,
+    up_send, down_send, side_send, above_send, below_send, note_send,
+):
+    me, t = lax.axis_index("dp"), lax.axis_index("tile")
+    z, x = me // across, me % across
+    owners = deep * across
+    has_above, has_below = t > 0, t < tiles - 1
+
+    barrier = pltpu.get_barrier_semaphore()
+
+    def greet(dp, tile):
+        pl.semaphore_signal(
+            barrier, inc=1, device_id=(dp, tile), device_id_type=pl.DeviceIdType.MESH
+        )
+
+    for j in range(1, owners):
+        greet((me + j) % owners, t)
+    pl.when(has_above)(lambda: greet(me, t - 1))
+    pl.when(has_below)(lambda: greet(me, t + 1))
+    pl.semaphore_wait(
+        barrier, owners - 1 + has_above.astype(jnp.int32) + has_below.astype(jnp.int32)
+    )
+
+    started = []
+
+    def launch(cond, make):
+        if cond is None:
+            make().start()
+        else:
+            pl.when(cond)(lambda: make().start())
+        started.append((cond, make))
+
+    def both(a, b):
+        if a is None:
+            return b
+        return a if b is None else jnp.logical_and(a, b)
+
+    def halos(cond, s, block):
+        launch(
+            both(cond, has_below),
+            lambda: remote(block, above_ref.at[s], above_send.at[s], above_recv.at[s], me, t + 1),
+        )
+        launch(
+            both(cond, has_above),
+            lambda: remote(block, below_ref.at[s], below_send.at[s], below_recv.at[s], me, t - 1),
+        )
+
+    def lift(cond, s, block):
+        launch(
+            both(cond, z < deep - 1),
+            lambda: remote(
+                block, rows_ref.at[s], up_send.at[s], main_recv.at[s], me + across, t
+            ),
+        )
+
+    def sink(cond, s, block):
+        launch(
+            both(cond, z > 0),
+            lambda: remote(
+                block, rows_ref.at[s], down_send.at[s], main_recv.at[s], me - across, t
+            ),
+        )
+
+    def side(cond, s, block):
+        for j in range(1, across):
+            launch(
+                cond,
+                lambda j=j: remote(
+                    block,
+                    rows_ref.at[s],
+                    side_send.at[j - 1, s],
+                    main_recv.at[s],
+                    z * across + (x + j) % across,
+                    t,
+                ),
+            )
+
+    def arrive(cond, s):
+        def wait():
+            remote(
+                rows_ref.at[s], rows_ref.at[s], up_send.at[s], main_recv.at[s], me, t
+            ).wait_recv()
+
+        pl.when(cond)(wait) if cond is not None else wait()
+
+    lift(None, me, own_ref)
+    sink(None, me, own_ref)
+    side(None, me, own_ref)
+    halos(None, me, own_ref.at[0])
+    for j in range(1, owners):
+        peer = (me + j) % owners
+        launch(
+            None,
+            lambda j=j, peer=peer: remote(
+                note_ref.at[peer], noted_ref.at[me], note_send.at[j - 1], note_recv.at[me], peer, t
+            ),
+        )
+    kept = pltpu.make_async_copy(own_ref, rows_ref.at[me], local_sem.at[0])
+    kept.start()
+    noted = pltpu.make_async_copy(note_ref.at[me], noted_ref.at[me], local_sem.at[1])
+    noted.start()
+
+    def side_arrivals(k):
+        for sign in (1, -1) if k else (1,):
+            zs = z - sign * k
+            cond = (zs >= 0 if sign > 0 else zs < deep) if k else None
+            for j in range(1, across):
+                s = zs * across + (x + j) % across
+                arrive(cond, s)
+                halos(cond, s, rows_ref.at[s, 0])
+
+    for k in range(1, deep):
+        lower, upper = z - k, z + k
+        s = lower * across + x
+        arrive(lower >= 0, s)
+        lift(lower >= 0, s, rows_ref.at[s])
+        side(lower >= 0, s, rows_ref.at[s])
+        halos(lower >= 0, s, rows_ref.at[s, 0])
+        s = upper * across + x
+        arrive(upper < deep, s)
+        sink(upper < deep, s, rows_ref.at[s])
+        side(upper < deep, s, rows_ref.at[s])
+        halos(upper < deep, s, rows_ref.at[s, 0])
+        side_arrivals(k - 1)
+    side_arrivals(deep - 1)
+
+    for j in range(1, owners):
+        s = (me + j) % owners
+        remote(
+            note_ref.at[s], noted_ref.at[s], note_send.at[j - 1], note_recv.at[s], s, t
+        ).wait_recv()
+    for s in range(owners):
+        pl.when(has_above)(
+            lambda s=s: remote(
+                above_ref.at[s], above_ref.at[s], above_send.at[s], above_recv.at[s], me, t
+            ).wait_recv()
+        )
+        pl.when(has_below)(
+            lambda s=s: remote(
+                below_ref.at[s], below_ref.at[s], below_send.at[s], below_recv.at[s], me, t
+            ).wait_recv()
+        )
+    for cond, make in started:
+        if cond is None:
+            make().wait_send()
+        else:
+            pl.when(cond)(lambda make=make: make().wait_send())
+    kept.wait()
+    noted.wait()
+
+
+def spread(own, note, owners, tiles):
+    deep, across = grid_of(owners)
+    dma = pltpu.SemaphoreType.DMA
+    anywhere = pl.BlockSpec(memory_space=pl.ANY)
+    return pl.pallas_call(
+        functools.partial(spread_kernel, deep, across, tiles),
+        out_shape=[
+            jax.ShapeDtypeStruct((owners,) + own.shape, own.dtype),
+            jax.ShapeDtypeStruct((owners,) + own.shape[1:], own.dtype),
+            jax.ShapeDtypeStruct((owners,) + own.shape[1:], own.dtype),
+            jax.ShapeDtypeStruct(note.shape, note.dtype),
+        ],
+        in_specs=[pl.BlockSpec(memory_space=pltpu.VMEM)] * 2,
+        out_specs=[anywhere] * 4,
+        scratch_shapes=[
+            dma((2,)), dma((owners,)), dma((owners,)), dma((owners,)), dma((owners,)),
+            dma((owners,)), dma((owners,)), dma((max(across - 1, 1), owners)),
+            dma((owners,)), dma((owners,)), dma((owners,)),
+        ],
+        compiler_params=pltpu.CompilerParams(
+            collective_id=0, has_side_effects=True, vmem_limit_bytes=8 * 1024 * 1024
+        ),
+        name="spread",
+    )(own, note)
 
 
 def swap(x):
@@ -132,10 +345,6 @@
     tiles = lax.axis_size("tile")
     local = kernels.shape[0]
     up, down = line(tiles)
-    before = lax.ppermute(frames[:, -1:], "tile", up)
-    after = lax.ppermute(frames[:, :1], "tile", down)
-    sheet = jnp.concatenate([before, frames, after, cotangent], axis=1)
-
     chosen = experts[:, 0]
     frame_count, slots = chosen.shape
     active = jnp.arange(slots)[None, :] < counts[:, 0][:, None]
@@ -149,18 +358,25 @@
     request = jnp.max(jnp.where(hit, (chosen % local)[:, :, None], 0), axis=(0, 1))
     tile_gate = jnp.sum(jnp.where(hit, gate_weights[:, 0][:, :, None], 0.0), axis=1)
     weight = jnp.sum(jnp.where(slot_map, tile_gate.T[:, None, :], 0.0), axis=2)
-    note = jnp.concatenate([request[:, None].astype(jnp.float32), weight], axis=1)
-    noted = swap(note)
+    place = jnp.sum(
+        jnp.where(slot_map, jnp.arange(frame_count)[None, None, :], 0), axis=2
+    )
+    note = jnp.concatenate(
+        [request[:, None].astype(jnp.float32), weight, place.astype(jnp.float32)], axis=1
+    )
+    note = jnp.pad(note[:, None, :], ((0, 0), (0, 7), (0, 128 - note.shape[1])))
+    own = jnp.stack([frames[:, 0], cotangent[:, 0]])
+    rows, above, below, noted = spread(own, note, owners, tiles)
+    noted = noted[:, 0]
     pick = noted[:, 0].astype(jnp.int32)
-    shares = noted[:, 1:]
-
-    picked = slot_map.astype(jnp.bfloat16).reshape(owners * CAP, frame_count)
-    outgoing = jnp.dot(
-        picked, sheet.reshape(frame_count, -1), preferred_element_type=jnp.float32
-    ).astype(jnp.bfloat16)
-    items = swap(outgoing.reshape((owners, CAP) + sheet.shape[1:]))
-
-    back, gates, bank_grad = owner(pick, shares, items, kernels, tiles)
+    shares = noted[:, 1 : 1 + CAP]
+    places = noted[:, 1 + CAP : 1 + 2 * CAP].astype(jnp.int32)
+    t = lax.axis_index("tile")
+    rim = jnp.stack([t > 0, t < tiles - 1]).astype(jnp.int32)
+
+    back, gates, bank_grad = owner(
+        pick, shares, places, rim, rows, above, below, kernels, tiles
+    )
     kernel_part = lax.psum_scatter(bank_grad, "tile", scatter_dimension=0, tiled=True)[0]
     kernel_part = jnp.swapaxes(kernel_part, 2, 3)
 
@@ -169,9 +385,10 @@
     selected = jnp.sum(jnp.where(slot_map, gates[:, :, None], 0.0), axis=1)
     gate_grad = jnp.sum(jnp.where(hit, selected.T[:, None, :], 0.0), axis=2)
 
+    picked = slot_map.astype(jnp.bfloat16).reshape(owners * CAP, frame_count)
     gathered = jnp.dot(
         picked.T, arrived.reshape(owners * CAP, -1), preferred_element_type=jnp.float32
-    ).reshape(sheet.shape)
+    ).reshape((frame_count,) + arrived.shape[2:])
     result = (frames.astype(jnp.float32) + gathered[:, 3:4]).astype(jnp.bfloat16)
     from_above = lax.ppermute(gathered[:, 2:3].astype(jnp.bfloat16), "tile", up)
     from_below = lax.ppermute(gathered[:, 0:1].astype(jnp.bfloat16), "tile", down)

time: 182 us -> 150 us (0.82)
  waiting for transfers between devices: 110 us -> 58.6 us
  Pallas kernels: 16 us -> 51.9 us
  starting transfers between devices: 24.6 us -> 10.3 us
    all_to_all x4 -> x2, waiting for transfers between devices: 99.4 us -> 48.3 us  [swap(): return lax.all_to_all(x, 'dp', split_axis=0, concat_axis=0, tiled=True)]
    pallas_call x0 -> x1, Pallas kernels: none -> 35.6 us  [spread(): pl.pallas_call(functools.partial(spread_kernel, deep, across, tiles), out...]
    all_to_all x4 -> x2, starting transfers between devices: 17.9 us -> 7.23 us  [swap(): return lax.all_to_all(x, 'dp', split_axis=0, concat_axis=0, tiled=True)]
    ppermute x2 -> x0, starting transfers between devices: 3.7 us -> none  [the longest x1 2.41 us: shards(): before = lax.ppermute(frames[:, -1:], 'tile', up)]
    unnamed x10 -> x9, local copies, waits for them, and re-layouts: 5.68 us -> 4.72 us
  transfers between devices with their start and end apart: 9 -> 5, of which waited for: 5 -> 3; matrix products, arithmetic and copies ran while one was open for 9% -> 6% of each run, Pallas kernels for 0% -> 0%
where the time goes in v2:
time: 150 us; the launch traced here: 149 us
  waiting for transfers between devices  58.6 us (39%)
  Pallas kernels  51.9 us (35%)
  between operations  14.2 us (9%)
  starting transfers between devices  10.3 us (7%)
  local copies, waits for them, and re-layouts  7.73 us (5%)
  other arithmetic  5.08 us (3%)
    all_to_all x2, waiting for transfers between devices, swap(): return lax.all_to_all(x, 'dp', split_axis=0, concat_axis=0, tiled=True)  48.3 us
    pallas_call x1, Pallas kernels, spread(): pl.pallas_call(functools.partial(spread_kernel, deep, across, tiles), out...  35.6 us
    pallas_call x1, Pallas kernels, owner(): pl.pallas_call(owner_kernel, grid_spec=spec, out_shape=[jax.ShapeDtypeStr...  16.3 us
    reduce_scatter x1, waiting for transfers between devices, shards(): lax.psum_scatter(bank_grad, 'tile', scatter_dimension=0, tiled=True)[0]  9.22 us
    all_to_all x2, starting transfers between devices, swap(): return lax.all_to_all(x, 'dp', split_axis=0, concat_axis=0, tiled=True)  7.23 us
    unnamed x9, local copies, waits for them, and re-layouts  4.72 us
  transfers between devices with their start and end apart: 5, of which 3 were waited for; matrix products, arithmetic and copies ran while one was open for 6% of the time, Pallas kernels for 0%

profile of v2, /device:TPU:0, one launch (start us, length us, event | category | flops | bytes accessed | tf_op | source)
XLA Modules:
  0.0 149.1 jit_solution(866802806579365660)
XLA Ops:
  7.2 0.7 add_select_fusion.1
  7.9 0.7 iota_compare_fusion.2
  8.8 0.8 select_reduce_fusion.4
  9.9 1.0 pad_maximum_fusion.own_ref
  10.9 35.6 %spread.1 = (bf16[8,2,4,64,256]{4,3,2,1,0:T(8,128)(2,1)S(1)}, bf16[8,4,64,256]{3,2,1,0:T(8,128)(2,1)S(1)}, bf16[8,4,64,256]{3,2,1,0:T(8,128)(2,1)S(1)}, f32[8,8,128]{2,1,0:T(8,128)S(1)}) custom-call(bf16[2,4,64,256]{3,2,1,0:T(8,128)(2,1)S(1)} %pad_maximum_fusion.own_ref, f32[8,8,128]{2,1,0:T(8,128)S(1)} %pad.4.note_ref), custom_call_target="tpu_custom_call" | custom-call | tf_op jit(solution)/shard_map/spread/pallas_call | solution.py:312
  46.5 1.3 copy-done
  47.9 0.1 convert_reduce_fusion.pick_ref
  48.1 16.3 %owner.1 = (bf16[8,2,4,64,256]{4,3,2,1,0:T(8,128)(2,1)}, f32[8,2,128]{2,1,0:T(2,128)S(1)}, f32[4,4,9,64,256]{4,3,2,1,0:T(8,128)}) custom-call(s32[8]{0:T(128)S(1)} %convert_reduce_fusion.pick_ref, f32[8,2]{1,0:T(8,128)S(1)} %get-tuple-element.41.weight_ref, s32[8,2]{1,0:T(8,128)S(1)} %get-tuple-element.40.place_ref, s32[2]{0:T(128)S(1)} %add_convert_fusion.rim_ref, ...), custom_call_target="tpu_custom_call" | custom-call | tf_op jit(solution)/shard_map/owner/pallas_call | solution.py:119
  64.5 3.6 %all-to-all-start = ((bf16[8,2,4,64,256]{4,3,2,1,0:T(8,128)(2,1)}), bf16[8,2,4,64,256]{4,3,2,1,0:T(8,128)(2,1)S(1)}, u32[]{:S(2)}, u32[]{:S(2)}) async-start(bf16[8,2,4,64,256]{4,3,2,1,0:T(8,128)(2,1)} %get-tuple-element.15), calls=%async_computation | async-start | bytes 4194304 | tf_op jit(solution)/shard_map/all_to_all | solution.py:335
  68.3 0.7 copy.51
  69.0 48.2 %all-to-all-done = bf16[8,2,4,64,256]{4,3,2,1,0:T(8,128)(2,1)S(1)} async-done(((bf16[8,2,4,64,256]{4,3,2,1,0:T(8,128)(2,1)}), bf16[8,2,4,64,256]{4,3,2,1,0:T(8,128)(2,1)S(1)}, u32[]{:S(2)}, u32[]{:S(2)}) %all-to-all-start) | async-done | bytes 2097184 | tf_op jit(solution)/shard_map/all_to_all | solution.py:335
  117.3 3.6 %all-to-all-start.1 = ((f32[8,1,2]{2,1,0:T(1,128)}), f32[8,1,2]{2,1,0:T(1,128)S(1)}, u32[]{:S(2)}, u32[]{:S(2)}) async-start(f32[8,1,2]{2,1,0:T(1,128)} %copy.51), calls=%async_computation.1 | async-start | bytes 8192 | tf_op jit(solution)/shard_map/all_to_all | solution.py:335
  120.9 2.0 %reshape.141 = bf16[16,65536]{1,0:T(8,128)(2,1)} reshape(bf16[8,2,4,64,256]{4,3,2,1,0:T(8,128)(2,1)S(1)} %all-to-all-done) | data formatting | bytes 4194304 | tf_op jit(solution)/shard_map/reshape | solution.py:390
  122.9 2.0 %copy.59 = bf16[2,8,256,256]{3,2,1,0:T(8,128)(2,1)S(1)} copy(bf16[2,8,256,256]{3,1,2,0:T(8,128)(2,1)} %bitcast.45) | data formatting | bytes 4194304
  124.9 1.4 fusion.12
  126.4 1.7 %collective-permute-start = (bf16[4,1,64,256]{3,0,2,1:T(4,128)(2,1)S(1)}, bf16[4,1,64,256]{3,0,2,1:T(4,128)(2,1)S(1)}, u32[]{:S(2)}, u32[]{:S(2)}) collective-permute-start(bf16[4,1,64,256]{3,0,2,1:T(4,128)(2,1)S(1)} %get-tuple-element.38), channel_id=1, source_target_pairs={{0,1},{1,2},{2,3},{4,5},{5,6},{6,7},{8,9},{9,10},{10,11},{12,13},{... | collective-permute-start | bytes 393224 | tf_op jit(solution)/shard_map/ppermute | solution.py:393
  128.1 1.3 collective-permute-start.1
  129.4 0.2 select_reduce_fusion
  129.6 0.7 select_reduce_fusion.3
  130.3 1.1 collective-permute-done.1
  131.4 0.3 fusion.4
  131.7 0.7 copy.54
  132.4 0.7 copy.55
  133.0 9.2 %reduce-scatter.2.cloned.1.call-done = f32[1,4,9,64,256]{4,3,2,1,0:T(8,128)} async-done(((f32[4,4,9,64,256]{4,3,2,1,0:T(8,128)}), f32[1,4,9,64,256]{4,3,2,1,0:T(8,128)}) %reduce-scatter.2.cloned.1.call-update) | async-done | bytes 2359312 | tf_op jit(solution)/shard_map/reduce_scatter | solution.py:380
  (29 shorter events, 1.1 us)
Async XLA Ops:
  7.2 135.1 %reduce-scatter.2.cloned.1.call-start = ((), (), s32[]{:S(2)}) async-start(), calls=%async_computation.3 | async-start | bytes 11796480 | tf_op jit(solution)/shard_map/reduce_scatter | solution.py:380
  46.5 1.3 copy-start
  64.5 52.8 %all-to-all-start = ((bf16[8,2,4,64,256]{4,3,2,1,0:T(8,128)(2,1)}), bf16[8,2,4,64,256]{4,3,2,1,0:T(8,128)(2,1)S(1)}, u32[]{:S(2)}, u32[]{:S(2)}) async-start(bf16[8,2,4,64,256]{4,3,2,1,0:T(8,128)(2,1)} %get-tuple-element.15), calls=%async_computation | async-start | bytes 4194304 | tf_op jit(solution)/shard_map/all_to_all | solution.py:335
  117.3 12.1 %all-to-all-start.1 = ((f32[8,1,2]{2,1,0:T(1,128)}), f32[8,1,2]{2,1,0:T(1,128)S(1)}, u32[]{:S(2)}, u32[]{:S(2)}) async-start(f32[8,1,2]{2,1,0:T(1,128)} %copy.51), calls=%async_computation.1 | async-start | bytes 8192 | tf_op jit(solution)/shard_map/all_to_all | solution.py:335
  124.9 6.5 %copy-start.1 = (bf16[4,1,64,256]{3,2,1,0:T(8,128)(2,1)S(1)}, bf16[4,1,64,256]{3,2,1,0:T(8,128)(2,1)}, u32[]{:S(2)}) copy-start(bf16[4,1,64,256]{3,2,1,0:T(8,128)(2,1)} %param.11) | copy-start | bytes 393220
  124.9 6.4 %copy-start.2 = (bf16[4,1,64,256]{3,2,1,0:T(8,128)(2,1)S(1)}, bf16[4,1,64,256]{3,2,1,0:T(8,128)(2,1)}, u32[]{:S(2)}) copy-start(bf16[4,1,64,256]{3,2,1,0:T(8,128)(2,1)} %param.6) | copy-start | bytes 393220
  126.4 3.9 %collective-permute-start = (bf16[4,1,64,256]{3,0,2,1:T(4,128)(2,1)S(1)}, bf16[4,1,64,256]{3,0,2,1:T(4,128)(2,1)S(1)}, u32[]{:S(2)}, u32[]{:S(2)}) collective-permute-start(bf16[4,1,64,256]{3,0,2,1:T(4,128)(2,1)S(1)} %get-tuple-element.38), channel_id=1, source_target_pairs={{0,1},{1,2},{2,3},{4,5},{5,6},{6,7},{8,9},{9,10},{10,11},{12,13},{... | collective-permute-start | bytes 393224 | tf_op jit(solution)/shard_map/ppermute | solution.py:393
  128.1 3.2 %collective-permute-start.1 = (bf16[4,1,64,256]{3,0,2,1:T(4,128)(2,1)S(1)}, bf16[4,1,64,256]{3,0,2,1:T(4,128)(2,1)S(1)}, u32[]{:S(2)}, u32[]{:S(2)}) collective-permute-start(bf16[4,1,64,256]{3,0,2,1:T(4,128)(2,1)S(1)} %get-tuple-element.39), channel_id=1, source_target_pairs={{1,0},{2,1},{3,2},{5,4},{6,5},{7,6},{9,8},{10,9},{11,10},{13,12},{... | collective-permute-start | bytes 393224 | tf_op jit(solution)/shard_map/ppermute | solution.py:394
Sparse Core Ops, SparseCore 0:
  64.6 77.6 reduce-scatter.1

commit v3 on v2

--- a/solution.py
+++ b/solution.py
@@ -24,16 +24,22 @@
 
 def owner_kernel(
     pick_ref, weight_ref, place_ref, rim_ref,
-    rows_ref, above_ref, below_ref, bank_ref, back_ref, gate_ref, grad_ref,
+    rows_ref, above_ref, below_ref, bank_ref, back_ref, gate_ref, out_ref, grad_ref,
 ):
     s = pl.program_id(0)
-    cap, _, columns, channels = back_ref.shape[1:]
+    cap = CAP
+    columns, channels = back_ref.shape[3:]
+    steps = out_ref.shape[1]
     rows = cap * columns
     later, sooner = shifts(columns, rows)
 
     @pl.when(s == 0)
     def _():
-        grad_ref[...] = jnp.zeros_like(grad_ref)
+        @pl.loop(0, steps)
+        def _(i):
+            grad_ref[:, i] = jnp.zeros_like(grad_ref[:, i])
+
+    back_ref[...] = jnp.zeros_like(back_ref)
 
     item = lax.broadcasted_iota(jnp.int32, (rows, 1), 0) // columns
     weight = jnp.zeros((rows, 1), jnp.float32)
@@ -64,9 +70,16 @@
     squash = jax.nn.sigmoid(pre)
     activated = pre * squash
     slope = squash * (1.0 + pre * (1.0 - squash))
-    back_ref[0, :, 3] = (weight * activated).astype(jnp.bfloat16).reshape(cap, columns, channels)
+
+    def put(r, value):
+        value = value.astype(jnp.bfloat16).reshape(cap, columns, channels)
+        for c in reversed(range(cap)):
+            back_ref[0, r, place_ref[s, c]] = value[c]
+
+    put(3, weight * activated)
     gates = jnp.sum((upstream * activated).reshape(cap, columns, channels), axis=1)
-    gate_ref[0] = jnp.broadcast_to(jnp.sum(gates, axis=1, keepdims=True), gate_ref.shape[1:])
+    gates = jnp.broadcast_to(jnp.sum(gates, axis=1, keepdims=True), (cap, 128))
+    gate_ref[0] = jnp.concatenate([gates, jnp.zeros((8 - cap, 128), jnp.float32)], axis=0)
 
     grad = (upstream * weight * slope).astype(jnp.bfloat16)
     for da in range(3):
@@ -80,18 +93,25 @@
             for db in range(3)
         ]
         total = parts[1] + sooner(parts[0]) + later(parts[2])
-        back_ref[0, :, da] = total.astype(jnp.bfloat16).reshape(cap, columns, channels)
+        put(da, total)
 
     grad_wide = grad.astype(jnp.float32)
     moved = [sooner(grad_wide).astype(jnp.bfloat16), grad, later(grad_wide).astype(jnp.bfloat16)]
     e = pick_ref[s]
-    chunks, _, _, share, _ = grad_ref.shape
+    chunks, _, share, _ = grad_ref.shape
+    taps = bank_ref.shape[1]
     for db in range(3):
         for da in range(3):
             term = lax.dot_general(
                 moved[db], window[da], (((0,), (0,)), ((), ())), preferred_element_type=jnp.float32
             )
-            grad_ref[:, e, 3 * da + db] += term.reshape(chunks, share, channels)
+            grad_ref[:, e * taps + 3 * da + db] += term.reshape(chunks, share, channels)
+
+    @pl.when(s == pl.num_programs(0) - 1)
+    def _():
+        @pl.loop(0, steps)
+        def _(i):
+            out_ref[:, i] = grad_ref[:, i].astype(out_ref.dtype)
 
 
 def owner(pick, weight, place, rim, rows, above, below, kernels, chunks):
@@ -107,23 +127,26 @@
             pl.BlockSpec((1, taps, channels, outputs), lambda s, p, *_: (p[s], 0, 0, 0)),
         ],
         out_specs=[
-            pl.BlockSpec((1, CAP, 4, columns, channels), lambda s, *_: (s, 0, 0, 0, 0)),
-            pl.BlockSpec((1, CAP, 128), lambda s, *_: (s, 0, 0)),
+            pl.BlockSpec((1, 4, frames, columns, channels), lambda s, *_: (s, 0, 0, 0, 0)),
+            pl.BlockSpec((1, 8, 128), lambda s, *_: (s, 0, 0)),
             pl.BlockSpec(
-                (chunks, experts, taps, outputs // chunks, channels),
-                lambda s, *_: (0, 0, 0, 0, 0),
+                (chunks, experts * taps, outputs // chunks, channels),
+                lambda s, *_: (0, 0, 0, 0),
                 pipeline_mode=pl.Buffered(1),
             ),
+        ],
+        scratch_shapes=[
+            pltpu.VMEM((chunks, experts * taps, outputs // chunks, channels), jnp.float32)
         ],
     )
     return pl.pallas_call(
         owner_kernel,
         grid_spec=spec,
         out_shape=[
-            jax.ShapeDtypeStruct((sources, CAP, 4, columns, channels), jnp.bfloat16),
-            jax.ShapeDtypeStruct((sources, CAP, 128), jnp.float32),
+            jax.ShapeDtypeStruct((sources, 4, frames, columns, channels), jnp.bfloat16),
+            jax.ShapeDtypeStruct((sources, 8, 128), jnp.float32),
             jax.ShapeDtypeStruct(
-                (chunks, experts, taps, outputs // chunks, channels), jnp.float32
+                (chunks, experts * taps, outputs // chunks, channels), jnp.bfloat16
             ),
         ],
         compiler_params=pltpu.CompilerParams(vmem_limit_bytes=48 * 1024 * 1024),
@@ -331,20 +354,287 @@
     )(own, note)
 
 
-def swap(x):
-    return lax.all_to_all(x, "dp", split_axis=0, concat_axis=0, tiled=True)
-
-
-def line(count):
-    up = [(i, i + 1) for i in range(count - 1)]
-    return up, [(j, i) for i, j in up]
+def collect_kernel(
+    deep, across, high, cores,
+    terms_ref, gate_ref, bank_ref, own_ref,
+    result_ref, input_ref, gated_ref, grad_ref,
+    above, below, side_out, side_in, far_out, far_in, total, mate_in, band_out, band_in,
+    local_sem, above_send, above_recv, below_send, below_recv,
+    side_send, side_recv, far_send, far_recv, mate_send, mate_recv, band_send, band_recv,
+    gate_send, gate_recv,
+):
+    me, t = lax.axis_index("dp"), lax.axis_index("tile")
+    z, x = me // across, me % across
+    y, core = t // cores, t % cores
+    owners, tiles = deep * across, high * cores
+    frames = own_ref.shape[1]
+    steps = grad_ref.shape[0]
+    has_above, has_below = t > 0, t < tiles - 1
+
+    barrier = pltpu.get_barrier_semaphore()
+    for j in range(1, owners):
+        pl.semaphore_signal(
+            barrier, device_id=((me + j) % owners, t), device_id_type=pl.DeviceIdType.MESH
+        )
+    for j in range(1, tiles):
+        pl.semaphore_signal(
+            barrier, device_id=(me, (t + j) % tiles), device_id_type=pl.DeviceIdType.MESH
+        )
+    pl.semaphore_wait(barrier, owners - 1 + tiles - 1)
+
+    started = []
+
+    def launch(make, cond=None):
+        if cond is None:
+            make().start()
+        else:
+            pl.when(cond)(lambda: make().start())
+        started.append((cond, make))
+
+    ring = [(z + k) % deep for k in list(range(1, deep)) + [0]]
+
+    def lower(s):
+        return remote(terms_ref.at[s, 2], above.at[s], above_send.at[s], above_recv.at[s], me, t + 1)
+
+    def upper(s):
+        return remote(terms_ref.at[s, 0], below.at[s], below_send.at[s], below_recv.at[s], me, t - 1)
+
+    for j in list(range(1, across)) + [0]:
+        for zs in ring:
+            s = zs * across + (x + j) % across
+            launch(lambda s=s: lower(s), has_below)
+            launch(lambda s=s: upper(s), has_above)
+
+    bands = [(y + k) % high for k in list(range(1, high)) + [0]]
+    for k, ys in enumerate(bands):
+        for j in range(1, cores):
+            mate = (core + j) % cores
+            launch(
+                lambda k=k, j=j, ys=ys, mate=mate: remote(
+                    bank_ref.at[ys * cores + mate],
+                    mate_in.at[k, j - 1],
+                    mate_send.at[k, j - 1],
+                    mate_recv.at[k, j - 1],
+                    me,
+                    y * cores + mate,
+                )
+            )
+    for j in range(1, owners):
+        peer = (me + j) % owners
+        launch(
+            lambda j=j, peer=peer: remote(
+                gate_ref.at[peer], gated_ref.at[me], gate_send.at[j - 1], gate_recv.at[j - 1], peer, t
+            )
+        )
+    kept = pltpu.make_async_copy(gate_ref.at[me], gated_ref.at[me], local_sem.at[0])
+    kept.start()
+
+    @pl.when(jnp.logical_not(has_above))
+    def _():
+        above[...] = jnp.zeros_like(above)
+
+    @pl.when(jnp.logical_not(has_below))
+    def _():
+        below[...] = jnp.zeros_like(below)
+
+    def rims(s):
+        pl.when(has_above)(
+            lambda: remote(
+                above.at[s], above.at[s], above_send.at[s], above_recv.at[s], me, t - 1
+            ).wait_recv()
+        )
+        pl.when(has_below)(
+            lambda: remote(
+                below.at[s], below.at[s], below_send.at[s], below_recv.at[s], me, t + 1
+            ).wait_recv()
+        )
+
+    def wide(ref, *at):
+        return ref[at].astype(jnp.float32)
+
+    def row(s, f):
+        return wide(terms_ref, s, 1, f) + wide(above, s, f) + wide(below, s, f)
+
+    for k, zs in enumerate(ring):
+        for j in range(1, across):
+            xs = (x + j) % across
+            s = zs * across + xs
+            rims(s)
+
+            @pl.loop(0, frames)
+            def _(f):
+                side_out[j - 1, k, 0, f] = row(s, f).astype(jnp.bfloat16)
+                side_out[j - 1, k, 1, f] = terms_ref[s, 3, f]
+
+            launch(
+                lambda k=k, j=j, xs=xs: remote(
+                    side_out.at[j - 1, k],
+                    side_in.at[j - 1, k],
+                    side_send.at[j - 1, k],
+                    side_recv.at[j - 1, k],
+                    z * across + xs,
+                    t,
+                )
+            )
+
+    for k, ys in enumerate(bands):
+        for j in range(1, cores):
+            remote(
+                mate_in.at[k, j - 1], mate_in.at[k, j - 1],
+                mate_send.at[k, j - 1], mate_recv.at[k, j - 1],
+                me, y * cores + (core + j) % cores,
+            ).wait_recv()
+        if k < high - 1:
+
+            @pl.loop(0, steps)
+            def _(i):
+                value = wide(bank_ref, ys * cores + core, i)
+                for j in range(1, cores):
+                    value = value + wide(mate_in, k, j - 1, i)
+                band_out[k, i] = value.astype(jnp.bfloat16)
+
+            launch(
+                lambda k=k, ys=ys: remote(
+                    band_out.at[k], band_in.at[k], band_send.at[k], band_recv.at[k],
+                    me, ys * cores + core,
+                )
+            )
+
+    for k, zs in enumerate(ring):
+        s = zs * across + x
+        rims(s)
+        for j in range(1, across):
+            remote(
+                side_in.at[j - 1, k], side_in.at[j - 1, k],
+                side_send.at[j - 1, k], side_recv.at[j - 1, k],
+                z * across + (x + j) % across, t,
+            ).wait_recv()
+
+        def summed(f):
+            first, second = row(s, f), wide(terms_ref, s, 3, f)
+            for j in range(1, across):
+                first = first + wide(side_in, j - 1, k, 0, f)
+                second = second + wide(side_in, j - 1, k, 1, f)
+            return first, second
+
+        if k < deep - 1:
+
+            @pl.loop(0, frames)
+            def _(f):
+                first, second = summed(f)
+                far_out[k, 0, f] = first.astype(jnp.bfloat16)
+                far_out[k, 1, f] = second.astype(jnp.bfloat16)
+
+            launch(
+                lambda k=k, zs=zs: remote(
+                    far_out.at[k], far_in.at[k], far_send.at[k], far_recv.at[k],
+                    zs * across + x, t,
+                )
+            )
+        else:
+
+            @pl.loop(0, frames)
+            def _(f):
+                first, second = summed(f)
+                total[0, f] = wide(own_ref, 1, f) + first
+                total[1, f] = wide(own_ref, 0, f) + second
+
+    for k in range(high - 1):
+        remote(
+            band_in.at[k], band_in.at[k], band_send.at[k], band_recv.at[k],
+            me, bands[k] * cores + core,
+        ).wait_recv()
+
+    @pl.loop(0, steps)
+    def _(i):
+        value = wide(bank_ref, t, i)
+        for j in range(1, cores):
+            value = value + wide(mate_in, high - 1, j - 1, i)
+        for k in range(high - 1):
+            value = value + wide(band_in, k, i)
+        grad_ref[i] = value
+
+    for k in range(deep - 1):
+        remote(
+            far_in.at[k], far_in.at[k], far_send.at[k], far_recv.at[k], ring[k] * across + x, t
+        ).wait_recv()
+
+    @pl.loop(0, frames)
+    def _(f):
+        first, second = total[0, f], total[1, f]
+        for k in range(deep - 1):
+            first = first + wide(far_in, k, 0, f)
+            second = second + wide(far_in, k, 1, f)
+        input_ref[f] = first.astype(jnp.bfloat16)
+        result_ref[f] = second.astype(jnp.bfloat16)
+
+    for j in range(1, owners):
+        s = (me + owners - j) % owners
+        remote(
+            gate_ref.at[s], gated_ref.at[s], gate_send.at[j - 1], gate_recv.at[j - 1], s, t
+        ).wait_recv()
+    for cond, make in started:
+        if cond is None:
+            make().wait_send()
+        else:
+            pl.when(cond)(lambda make=make: make().wait_send())
+    kept.wait()
+
+
+def collect(terms, gates, bank, own):
+    owners, _, frames, columns, channels = terms.shape
+    tiles, steps, share, _ = bank.shape
+    deep, across = grid_of(owners)
+    cores = 1 if tiles % 2 else 2
+    high = tiles // cores
+    dma = pltpu.SemaphoreType.DMA
+    vmem = pl.BlockSpec(memory_space=pltpu.VMEM)
+    beside, past, mates, far = (max(v - 1, 1) for v in (across, deep, cores, high))
+    block = (2, frames, columns, channels)
+
+    def room(*shape):
+        return pltpu.VMEM(shape, jnp.bfloat16)
+
+    return pl.pallas_call(
+        functools.partial(collect_kernel, deep, across, high, cores),
+        out_shape=[
+            jax.ShapeDtypeStruct(block[1:], jnp.bfloat16),
+            jax.ShapeDtypeStruct(block[1:], jnp.bfloat16),
+            jax.ShapeDtypeStruct(gates.shape, gates.dtype),
+            jax.ShapeDtypeStruct(bank.shape[1:], jnp.float32),
+        ],
+        in_specs=[vmem] * 4,
+        out_specs=[vmem] * 4,
+        scratch_shapes=[
+            room(owners, *block[1:]),
+            room(owners, *block[1:]),
+            room(beside, deep, *block),
+            room(beside, deep, *block),
+            room(past, *block),
+            room(past, *block),
+            pltpu.VMEM(block, jnp.float32),
+            room(high, mates, steps, share, channels),
+            room(far, steps, share, channels),
+            room(far, steps, share, channels),
+            dma((1,)),
+            dma((owners,)), dma((owners,)), dma((owners,)), dma((owners,)),
+            dma((beside, deep)), dma((beside, deep)),
+            dma((past,)), dma((past,)),
+            dma((high, mates)), dma((high, mates)),
+            dma((far,)), dma((far,)),
+            dma((max(owners - 1, 1),)), dma((max(owners - 1, 1),)),
+        ],
+        compiler_params=pltpu.CompilerParams(
+            collective_id=1, has_side_effects=True, vmem_limit_bytes=56 * 1024 * 1024
+        ),
+        name="collect",
+    )(terms, gates, bank, own)
 
 
 def shards(frames, kernels, experts, counts, gate_weights, cotangent):
     owners = lax.axis_size("dp")
     tiles = lax.axis_size("tile")
     local = kernels.shape[0]
-    up, down = line(tiles)
     chosen = experts[:, 0]
     frame_count, slots = chosen.shape
     active = jnp.arange(slots)[None, :] < counts[:, 0][:, None]
@@ -377,28 +667,14 @@
     back, gates, bank_grad = owner(
         pick, shares, places, rim, rows, above, below, kernels, tiles
     )
-    kernel_part = lax.psum_scatter(bank_grad, "tile", scatter_dimension=0, tiled=True)[0]
-    kernel_part = jnp.swapaxes(kernel_part, 2, 3)
-
-    arrived = swap(back)
-    gates = swap(gates[:, :, 0])
-    selected = jnp.sum(jnp.where(slot_map, gates[:, :, None], 0.0), axis=1)
+    result, input_grad, gated, bank_part = collect(back, gates, bank_grad, own)
+    kernel_part = jnp.swapaxes(bank_part, 1, 2).reshape(
+        kernels.shape[:3] + (bank_part.shape[1],)
+    )
+    gated = gated[:, :CAP, 0]
+    selected = jnp.sum(jnp.where(slot_map, gated[:, :, None], 0.0), axis=1)
     gate_grad = jnp.sum(jnp.where(hit, selected.T[:, None, :], 0.0), axis=2)
-
-    picked = slot_map.astype(jnp.bfloat16).reshape(owners * CAP, frame_count)
-    gathered = jnp.dot(
-        picked.T, arrived.reshape(owners * CAP, -1), preferred_element_type=jnp.float32
-    ).reshape((frame_count,) + arrived.shape[2:])
-    result = (frames.astype(jnp.float32) + gathered[:, 3:4]).astype(jnp.bfloat16)
-    from_above = lax.ppermute(gathered[:, 2:3].astype(jnp.bfloat16), "tile", up)
-    from_below = lax.ppermute(gathered[:, 0:1].astype(jnp.bfloat16), "tile", down)
-    input_grad = (
-        cotangent.astype(jnp.float32)
-        + gathered[:, 1:2]
-        + from_above.astype(jnp.float32)
-        + from_below.astype(jnp.float32)
-    ).astype(jnp.bfloat16)
-    return (result, input_grad, gate_grad[:, None, :], kernel_part)
+    return (result[:, None], input_grad[:, None], gate_grad[:, None, :], kernel_part)
 
 
 def solution(mesh):

time: 150 us -> 112 us (0.75)
  waiting for transfers between devices: 58.6 us -> 0 us
  Pallas kernels: 51.9 us -> 98.5 us
  between operations: 14.2 us -> 0.71 us
  starting transfers between devices: 10.3 us -> 0 us
    all_to_all x2 -> x0, waiting for transfers between devices: 48.3 us -> none  [swap(): return lax.all_to_all(x, 'dp', split_axis=0, concat_axis=0, tiled=True)]
    pallas_call x0 -> x1, Pallas kernels: none -> 47 us  [collect(): pl.pallas_call(functools.partial(collect_kernel, deep, across, high, core...]
    reduce_scatter x1 -> x0, waiting for transfers between devices: 9.22 us -> none  [shards(): lax.psum_scatter(bank_grad, 'tile', scatter_dimension=0, tiled=True)[0]]
    all_to_all x2 -> x0, starting transfers between devices: 7.23 us -> none  [swap(): return lax.all_to_all(x, 'dp', split_axis=0, concat_axis=0, tiled=True)]
    ppermute x2 -> x0, starting transfers between devices: 3.01 us -> none  [the longest x1 1.71 us: shards(): from_above = lax.ppermute(gathered[:, 2:3].astype(jnp.bfloat16), 'tile', up)]
    unnamed x9 -> x7, local copies, waits for them, and re-layouts: 4.72 us -> 7.07 us
    reshape x1 -> x0, local copies, waits for them, and re-layouts: 1.96 us -> none  [shards(): arrived.reshape(owners * CAP, -1)]
  transfers between devices with their start and end apart: 5 -> 0, of which waited for: 3 -> 0; matrix products, arithmetic and copies ran while one was open for 6% -> 0% of each run, Pallas kernels for 0% -> 0%
where the time goes in v3:
time: 112 us
  Pallas kernels  98.5 us (88%)
  local copies, waits for them, and re-layouts  8.03 us (7%)
  other arithmetic  4.36 us (4%)
    pallas_call x1, Pallas kernels, collect(): pl.pallas_call(functools.partial(collect_kernel, deep, across, high, core...  47 us
    pallas_call x1, Pallas kernels, spread(): pl.pallas_call(functools.partial(spread_kernel, deep, across, tiles), out...  35.6 us
    pallas_call x1, Pallas kernels, owner(): pl.pallas_call(owner_kernel, grid_spec=spec, out_shape=[jax.ShapeDtypeStr...  15.9 us
    unnamed x7, local copies, waits for them, and re-layouts  7.07 us

profile of v3, /device:TPU:0, one launch (start us, length us, event | category | flops | bytes accessed | tf_op | source)
XLA Modules:
  0.0 111.6 jit_solution(10594400293089382464)
XLA Ops:
  0.6 0.1 add_convert_fusion.rim_ref
  0.7 0.7 iota_compare_fusion.2
  1.4 0.7 add_select_fusion.1
  2.1 0.1 select_reduce_fusion.2
  2.3 0.8 select_reduce_fusion.1
  3.2 0.1 copy.31
  3.2 1.0 pad_maximum_fusion.own_ref
  4.2 0.0 copy-start
  4.3 35.6 %spread.1 = (bf16[8,2,4,64,256]{4,3,2,1,0:T(8,128)(2,1)S(1)}, bf16[8,4,64,256]{3,2,1,0:T(8,128)(2,1)S(1)}, bf16[8,4,64,256]{3,2,1,0:T(8,128)(2,1)S(1)}, f32[8,8,128]{2,1,0:T(8,128)S(1)}) custom-call(bf16[2,4,64,256]{3,2,1,0:T(8,128)(2,1)S(1)} %pad_maximum_fusion.own_ref, f32[8,8,128]{2,1,0:T(8,128)S(1)} %pad.4.note_ref), custom_call_target="tpu_custom_call" | custom-call | tf_op jit(solution)/shard_map/spread/pallas_call | solution.py:335
  39.9 0.1 convert_reduce_fusion.pick_ref
  40.0 0.1 slice_convert_fusion
  40.1 15.9 %owner.1 = (bf16[8,4,4,64,256]{4,3,2,1,0:T(8,128)(2,1)}, f32[8,8,128]{2,1,0:T(8,128)S(1)}, bf16[4,36,64,256]{3,2,1,0:T(8,128)(2,1)}) custom-call(s32[8]{0:T(128)S(1)} %convert_reduce_fusion.pick_ref, f32[8,2]{1,0:T(8,128)S(1)} %get-tuple-element.43.weight_ref, s32[8,2]{1,0:T(8,128)S(1)} %get-tuple-element.42.place_ref, s32[2]{0:T(128)S(1)} %add_convert_fusion.rim_ref, ...), custom_call_target="tpu_custom_call" | custom-call | tf_op jit(solution)/shard_map/owner/pallas_call | solution.py:142
  56.0 0.0 copy-done
  56.0 0.0 copy-start.1
  56.0 0.6 copy-done.1
  56.6 47.0 %collect.1 = (bf16[4,64,256]{2,1,0:T(8,128)(2,1)}, bf16[4,64,256]{2,1,0:T(8,128)(2,1)}, f32[8,8,128]{2,1,0:T(8,128)}, f32[36,64,256]{2,1,0:T(8,128)}) custom-call(bf16[8,4,4,64,256]{4,3,2,1,0:T(8,128)(2,1)} %get-tuple-element.19.terms_ref, f32[8,8,128]{2,1,0:T(8,128)} %copy-done.1, bf16[4,36,64,256]{3,2,1,0:T(8,128)(2,1)} %get-tuple-element.21.bank_ref, ...), custom_call_target="tpu_custom_call" | custom-call | tf_op jit(solution)/shard_map/collect/pallas_call | solution.py:598
  103.6 0.8 slice.19
  104.4 0.1 copy.33
  104.5 0.7 select_reduce_fusion
  105.2 1.6 %copy.42 = bf16[4,1,64,256]{3,2,1,0:T(8,128)(2,1)} copy(bf16[4,1,64,256]{3,2,1,0:T(8,128)(2,1)} %bitcast.33) | data formatting | bytes 262144
  106.7 1.6 %copy.43 = bf16[4,1,64,256]{3,2,1,0:T(8,128)(2,1)} copy(bf16[4,1,64,256]{3,2,1,0:T(8,128)(2,1)} %bitcast.32) | data formatting | bytes 262144
  108.3 3.3 %copy.44 = f32[4,9,256,64]{2,3,1,0:T(8,128)} copy(f32[4,9,256,64]{2,3,1,0:T(8,128)} %bitcast.31) | data formatting | bytes 4718592
  (13 shorter events, 0.2 us)
Async XLA Ops:
  4.2 51.8 %copy-start = (bf16[2,4,64,256]{3,2,1,0:T(8,128)(2,1)}, bf16[2,4,64,256]{3,2,1,0:T(8,128)(2,1)S(1)}, u32[]{:S(2)}) copy-start(bf16[2,4,64,256]{3,2,1,0:T(8,128)(2,1)S(1)} %pad_maximum_fusion.own_ref) | copy-start | bytes 786436
  56.0 0.6 copy-start.1

commit v4 on v3

--- a/solution.py
+++ b/solution.py
@@ -224,48 +224,47 @@
             lambda: remote(block, below_ref.at[s], below_send.at[s], below_recv.at[s], me, t - 1),
         )
 
-    def lift(cond, s, block):
+    def lift(cond, s, part, block):
         launch(
             both(cond, z < deep - 1),
             lambda: remote(
-                block, rows_ref.at[s], up_send.at[s], main_recv.at[s], me + across, t
+                block, rows_ref.at[s, part], up_send.at[part, s], main_recv.at[part, s],
+                me + across, t,
             ),
         )
 
-    def sink(cond, s, block):
+    def sink(cond, s, part, block):
         launch(
             both(cond, z > 0),
             lambda: remote(
-                block, rows_ref.at[s], down_send.at[s], main_recv.at[s], me - across, t
+                block, rows_ref.at[s, part], down_send.at[part, s], main_recv.at[part, s],
+                me - across, t,
             ),
         )
 
-    def side(cond, s, block):
+    def side(cond, s, part, block):
         for j in range(1, across):
             launch(
                 cond,
                 lambda j=j: remote(
                     block,
-                    rows_ref.at[s],
-                    side_send.at[j - 1, s],
-                    main_recv.at[s],
+                    rows_ref.at[s, part],
+                    side_send.at[j - 1, part, s],
+                    main_recv.at[part, s],
                     z * across + (x + j) % across,
                     t,
                 ),
             )
 
-    def arrive(cond, s):
+    def arrive(cond, s, part):
         def wait():
             remote(
-                rows_ref.at[s], rows_ref.at[s], up_send.at[s], main_recv.at[s], me, t
+                rows_ref.at[s, part], rows_ref.at[s, part], up_send.at[part, s],
+                main_recv.at[part, s], me, t,
             ).wait_recv()
 
         pl.when(cond)(wait) if cond is not None else wait()
 
-    lift(None, me, own_ref)
-    sink(None, me, own_ref)
-    side(None, me, own_ref)
-    halos(None, me, own_ref.at[0])
     for j in range(1, owners):
         peer = (me + j) % owners
         launch(
@@ -274,34 +273,40 @@
                 note_ref.at[peer], noted_ref.at[me], note_send.at[j - 1], note_recv.at[me], peer, t
             ),
         )
+    for part in range(2):
+        lift(None, me, part, own_ref.at[part])
+        sink(None, me, part, own_ref.at[part])
+        side(None, me, part, own_ref.at[part])
+        if part == 0:
+            halos(None, me, own_ref.at[0])
     kept = pltpu.make_async_copy(own_ref, rows_ref.at[me], local_sem.at[0])
     kept.start()
     noted = pltpu.make_async_copy(note_ref.at[me], noted_ref.at[me], local_sem.at[1])
     noted.start()
 
-    def side_arrivals(k):
+    def side_arrivals(k, part):
         for sign in (1, -1) if k else (1,):
             zs = z - sign * k
             cond = (zs >= 0 if sign > 0 else zs < deep) if k else None
             for j in range(1, across):
                 s = zs * across + (x + j) % across
-                arrive(cond, s)
-                halos(cond, s, rows_ref.at[s, 0])
+                arrive(cond, s, part)
+                if part == 0:
+                    halos(cond, s, rows_ref.at[s, 0])
 
     for k in range(1, deep):
         lower, upper = z - k, z + k
-        s = lower * across + x
-        arrive(lower >= 0, s)
-        lift(lower >= 0, s, rows_ref.at[s])
-        side(lower >= 0, s, rows_ref.at[s])
-        halos(lower >= 0, s, rows_ref.at[s, 0])
-        s = upper * across + x
-        arrive(upper < deep, s)
-        sink(upper < deep, s, rows_ref.at[s])
-        side(upper < deep, s, rows_ref.at[s])
-        halos(upper < deep, s, rows_ref.at[s, 0])
-        side_arrivals(k - 1)
-    side_arrivals(deep - 1)
+        for part in range(2):
+            for zs, cond, onward in ((lower, lower >= 0, lift), (upper, upper < deep, sink)):
+                s = zs * across + x
+                arrive(cond, s, part)
+                onward(cond, s, part, rows_ref.at[s, part])
+                side(cond, s, part, rows_ref.at[s, part])
+                if part == 0:
+                    halos(cond, s, rows_ref.at[s, 0])
+            side_arrivals(k - 1, part)
+    for part in range(2):
+        side_arrivals(deep - 1, part)
 
     for j in range(1, owners):
         s = (me + j) % owners
@@ -343,8 +348,8 @@
         in_specs=[pl.BlockSpec(memory_space=pltpu.VMEM)] * 2,
         out_specs=[anywhere] * 4,
         scratch_shapes=[
-            dma((2,)), dma((owners,)), dma((owners,)), dma((owners,)), dma((owners,)),
-            dma((owners,)), dma((owners,)), dma((max(across - 1, 1), owners)),
+            dma((2,)), dma((2, owners)), dma((owners,)), dma((owners,)), dma((owners,)),
+            dma((2, owners)), dma((2, owners)), dma((max(across - 1, 1), 2, owners)),
             dma((owners,)), dma((owners,)), dma((owners,)),
         ],
         compiler_params=pltpu.CompilerParams(

time: 112 us -> 109 us (0.973)
  Pallas kernels: 98.5 us -> 95.7 us
    pallas_call x1, Pallas kernels: 35.6 us -> 31 us  [spread(): pl.pallas_call(functools.partial(spread_kernel, deep, across, tiles), out...]
    pallas_call x1, Pallas kernels: 47 us -> 48.9 us  [collect(): pl.pallas_call(functools.partial(collect_kernel, deep, across, high, core...]
where the time goes in v4:
time: 109 us
  Pallas kernels  95.7 us (88%)
  local copies, waits for them, and re-layouts  8.03 us (7%)
  other arithmetic  4.36 us (4%)
    pallas_call x1, Pallas kernels, collect(): pl.pallas_call(functools.partial(collect_kernel, deep, across, high, core...  48.9 us
    pallas_call x1, Pallas kernels, spread(): pl.pallas_call(functools.partial(spread_kernel, deep, across, tiles), out...  31 us
    pallas_call x1, Pallas kernels, owner(): pl.pallas_call(owner_kernel, grid_spec=spec, out_shape=[jax.ShapeDtypeStr...  15.8 us
    unnamed x7, local copies, waits for them, and re-layouts  7.07 us

profile of v4, /device:TPU:0, one launch (start us, length us, event | category | flops | bytes accessed | tf_op | source)
XLA Modules:
  0.0 108.8 jit_solution(17213733537312584086)
XLA Ops:
  0.6 0.1 add_convert_fusion.rim_ref
  0.7 0.7 iota_compare_fusion.2
  1.4 0.7 add_select_fusion.1
  2.1 0.1 select_reduce_fusion.2
  2.3 0.8 select_reduce_fusion.1
  3.2 0.1 copy.31
  3.2 1.0 pad_maximum_fusion.own_ref
  4.2 0.0 copy-start
  4.3 31.0 %spread.1 = (bf16[8,2,4,64,256]{4,3,2,1,0:T(8,128)(2,1)S(1)}, bf16[8,4,64,256]{3,2,1,0:T(8,128)(2,1)S(1)}, bf16[8,4,64,256]{3,2,1,0:T(8,128)(2,1)S(1)}, f32[8,8,128]{2,1,0:T(8,128)S(1)}) custom-call(bf16[2,4,64,256]{3,2,1,0:T(8,128)(2,1)S(1)} %pad_maximum_fusion.own_ref, f32[8,8,128]{2,1,0:T(8,128)S(1)} %pad.4.note_ref), custom_call_target="tpu_custom_call" | custom-call | tf_op jit(solution)/shard_map/spread/pallas_call | solution.py:340
  35.3 0.1 convert_reduce_fusion.pick_ref
  35.4 0.1 slice_convert_fusion
  35.5 15.8 %owner.1 = (bf16[8,4,4,64,256]{4,3,2,1,0:T(8,128)(2,1)}, f32[8,8,128]{2,1,0:T(8,128)S(1)}, bf16[4,36,64,256]{3,2,1,0:T(8,128)(2,1)}) custom-call(s32[8]{0:T(128)S(1)} %convert_reduce_fusion.pick_ref, f32[8,2]{1,0:T(8,128)S(1)} %get-tuple-element.43.weight_ref, s32[8,2]{1,0:T(8,128)S(1)} %get-tuple-element.42.place_ref, s32[2]{0:T(128)S(1)} %add_convert_fusion.rim_ref, ...), custom_call_target="tpu_custom_call" | custom-call | tf_op jit(solution)/shard_map/owner/pallas_call | solution.py:142
  51.3 0.0 copy-done
  51.3 0.0 copy-start.1
  51.3 0.6 copy-done.1
  51.9 48.9 %collect.1 = (bf16[4,64,256]{2,1,0:T(8,128)(2,1)}, bf16[4,64,256]{2,1,0:T(8,128)(2,1)}, f32[8,8,128]{2,1,0:T(8,128)}, f32[36,64,256]{2,1,0:T(8,128)}) custom-call(bf16[8,4,4,64,256]{4,3,2,1,0:T(8,128)(2,1)} %get-tuple-element.19.terms_ref, f32[8,8,128]{2,1,0:T(8,128)} %copy-done.1, bf16[4,36,64,256]{3,2,1,0:T(8,128)(2,1)} %get-tuple-element.21.bank_ref, ...), custom_call_target="tpu_custom_call" | custom-call | tf_op jit(solution)/shard_map/collect/pallas_call | solution.py:603
  100.8 0.8 slice.19
  101.5 0.1 copy.33
  101.7 0.7 select_reduce_fusion
  102.3 1.6 %copy.42 = bf16[4,1,64,256]{3,2,1,0:T(8,128)(2,1)} copy(bf16[4,1,64,256]{3,2,1,0:T(8,128)(2,1)} %bitcast.33) | data formatting | bytes 262144
  103.9 1.6 %copy.43 = bf16[4,1,64,256]{3,2,1,0:T(8,128)(2,1)} copy(bf16[4,1,64,256]{3,2,1,0:T(8,128)(2,1)} %bitcast.32) | data formatting | bytes 262144
  105.5 3.3 %copy.44 = f32[4,9,256,64]{2,3,1,0:T(8,128)} copy(f32[4,9,256,64]{2,3,1,0:T(8,128)} %bitcast.31) | data formatting | bytes 4718592
  (13 shorter events, 0.2 us)
Async XLA Ops:
  4.2 47.0 %copy-start = (bf16[2,4,64,256]{3,2,1,0:T(8,128)(2,1)}, bf16[2,4,64,256]{3,2,1,0:T(8,128)(2,1)S(1)}, u32[]{:S(2)}) copy-start(bf16[2,4,64,256]{3,2,1,0:T(8,128)(2,1)S(1)} %pad_maximum_fusion.own_ref) | copy-start | bytes 786436
  51.3 0.6 copy-start.1

commit v5 on v4

--- a/solution.py
+++ b/solution.py
@@ -24,7 +24,7 @@
 
 def owner_kernel(
     pick_ref, weight_ref, place_ref, rim_ref,
-    rows_ref, above_ref, below_ref, bank_ref, back_ref, gate_ref, out_ref, grad_ref,
+    rows_ref, above_ref, below_ref, bank_ref, back_ref, edge_ref, gate_ref, out_ref, grad_ref,
 ):
     s = pl.program_id(0)
     cap = CAP
@@ -76,7 +76,7 @@
         for c in reversed(range(cap)):
             back_ref[0, r, place_ref[s, c]] = value[c]
 
-    put(3, weight * activated)
+    put(1, weight * activated)
     gates = jnp.sum((upstream * activated).reshape(cap, columns, channels), axis=1)
     gates = jnp.broadcast_to(jnp.sum(gates, axis=1, keepdims=True), (cap, 128))
     gate_ref[0] = jnp.concatenate([gates, jnp.zeros((8 - cap, 128), jnp.float32)], axis=0)
@@ -93,7 +93,10 @@
             for db in range(3)
         ]
         total = parts[1] + sooner(parts[0]) + later(parts[2])
-        put(da, total)
+        if da == 1:
+            put(0, total)
+        else:
+            edge_ref[0, da // 2] = total.astype(jnp.bfloat16).reshape(cap, columns, channels)
 
     grad_wide = grad.astype(jnp.float32)
     moved = [sooner(grad_wide).astype(jnp.bfloat16), grad, later(grad_wide).astype(jnp.bfloat16)]
@@ -127,7 +130,8 @@
             pl.BlockSpec((1, taps, channels, outputs), lambda s, p, *_: (p[s], 0, 0, 0)),
         ],
         out_specs=[
-            pl.BlockSpec((1, 4, frames, columns, channels), lambda s, *_: (s, 0, 0, 0, 0)),
+            pl.BlockSpec((1, 2, frames, columns, channels), lambda s, *_: (s, 0, 0, 0, 0)),
+            pl.BlockSpec((1, 2, CAP, columns, channels), lambda s, *_: (s, 0, 0, 0, 0)),
             pl.BlockSpec((1, 8, 128), lambda s, *_: (s, 0, 0)),
             pl.BlockSpec(
                 (chunks, experts * taps, outputs // chunks, channels),
@@ -143,7 +147,8 @@
         owner_kernel,
         grid_spec=spec,
         out_shape=[
-            jax.ShapeDtypeStruct((sources, 4, frames, columns, channels), jnp.bfloat16),
+            jax.ShapeDtypeStruct((sources, 2, frames, columns, channels), jnp.bfloat16),
+            jax.ShapeDtypeStruct((sources, 2, CAP, columns, channels), jnp.bfloat16),
             jax.ShapeDtypeStruct((sources, 8, 128), jnp.float32),
             jax.ShapeDtypeStruct(
                 (chunks, experts * taps, outputs // chunks, channels), jnp.bfloat16
@@ -361,12 +366,12 @@
 
 def collect_kernel(
     deep, across, high, cores,
-    terms_ref, gate_ref, bank_ref, own_ref,
+    terms_ref, edge_ref, note_ref, gate_ref, bank_ref, own_ref,
     result_ref, input_ref, gated_ref, grad_ref,
-    above, below, side_out, side_in, far_out, far_in, total, mate_in, band_out, band_in,
+    above, below, above_note, below_note, side_out, side_in, far_out, far_in, total, mate_in, band_out, band_in,
     local_sem, above_send, above_recv, below_send, below_recv,
     side_send, side_recv, far_send, far_recv, mate_send, mate_recv, band_send, band_recv,
-    gate_send, gate_recv,
+    gate_send, gate_recv, tell_send, tell_recv,
 ):
     me, t = lax.axis_index("dp"), lax.axis_index("tile")
     z, x = me // across, me % across
@@ -399,11 +404,19 @@
     ring = [(z + k) % deep for k in list(range(1, deep)) + [0]]
 
     def lower(s):
-        return remote(terms_ref.at[s, 2], above.at[s], above_send.at[s], above_recv.at[s], me, t + 1)
+        return remote(edge_ref.at[s, 1], above.at[s], above_send.at[s], above_recv.at[s], me, t + 1)
 
     def upper(s):
-        return remote(terms_ref.at[s, 0], below.at[s], below_send.at[s], below_recv.at[s], me, t - 1)
-
+        return remote(edge_ref.at[s, 0], below.at[s], below_send.at[s], below_recv.at[s], me, t - 1)
+
+    def tell_lower():
+        return remote(note_ref, above_note, tell_send.at[0], tell_recv.at[0], me, t + 1)
+
+    def tell_upper():
+        return remote(note_ref, below_note, tell_send.at[1], tell_recv.at[1], me, t - 1)
+
+    launch(tell_lower, has_below)
+    launch(tell_upper, has_above)
     for j in list(range(1, across)) + [0]:
         for zs in ring:
             s = zs * across + (x + j) % across
@@ -437,10 +450,23 @@
     @pl.when(jnp.logical_not(has_above))
     def _():
         above[...] = jnp.zeros_like(above)
+        above_note[...] = jnp.zeros_like(above_note)
 
     @pl.when(jnp.logical_not(has_below))
     def _():
         below[...] = jnp.zeros_like(below)
+        below_note[...] = jnp.zeros_like(below_note)
+
+    pl.when(has_above)(
+        lambda: remote(
+            above_note, above_note, tell_send.at[0], tell_recv.at[0], me, t - 1
+        ).wait_recv()
+    )
+    pl.when(has_below)(
+        lambda: remote(
+            below_note, below_note, tell_send.at[1], tell_recv.at[1], me, t + 1
+        ).wait_recv()
+    )
 
     def rims(s):
         pl.when(has_above)(
@@ -458,7 +484,14 @@
         return ref[at].astype(jnp.float32)
 
     def row(s, f):
-        return wide(terms_ref, s, 1, f) + wide(above, s, f) + wide(below, s, f)
+        value = wide(terms_ref, s, 0, f)
+        for note, items in ((above_note, above), (below_note, below)):
+            for c in range(CAP):
+                place = note[s, c : c + 1, :]
+                place = jnp.concatenate([place] * (value.shape[1] // place.shape[1]), axis=1)
+                here = jnp.broadcast_to(place, value.shape) == f.astype(jnp.float32)
+                value = value + jnp.where(here, wide(items, s, c), 0.0)
+        return value
 
     for k, zs in enumerate(ring):
         for j in range(1, across):
@@ -469,7 +502,7 @@
             @pl.loop(0, frames)
             def _(f):
                 side_out[j - 1, k, 0, f] = row(s, f).astype(jnp.bfloat16)
-                side_out[j - 1, k, 1, f] = terms_ref[s, 3, f]
+                side_out[j - 1, k, 1, f] = terms_ref[s, 1, f]
 
             launch(
                 lambda k=k, j=j, xs=xs: remote(
@@ -516,7 +549,7 @@
             ).wait_recv()
 
         def summed(f):
-            first, second = row(s, f), wide(terms_ref, s, 3, f)
+            first, second = row(s, f), wide(terms_ref, s, 1, f)
             for j in range(1, across):
                 first = first + wide(side_in, j - 1, k, 0, f)
                 second = second + wide(side_in, j - 1, k, 1, f)
@@ -586,7 +619,7 @@
     kept.wait()
 
 
-def collect(terms, gates, bank, own):
+def collect(terms, edges, notes, gates, bank, own):
     owners, _, frames, columns, channels = terms.shape
     tiles, steps, share, _ = bank.shape
     deep, across = grid_of(owners)
@@ -608,11 +641,13 @@
             jax.ShapeDtypeStruct(gates.shape, gates.dtype),
             jax.ShapeDtypeStruct(bank.shape[1:], jnp.float32),
         ],
-        in_specs=[vmem] * 4,
+        in_specs=[vmem] * 6,
         out_specs=[vmem] * 4,
         scratch_shapes=[
-            room(owners, *block[1:]),
-            room(owners, *block[1:]),
+            room(owners, *edges.shape[2:]),
+            room(owners, *edges.shape[2:]),
+            pltpu.VMEM(notes.shape, jnp.float32),
+            pltpu.VMEM(notes.shape, jnp.float32),
             room(beside, deep, *block),
             room(beside, deep, *block),
             room(past, *block),
@@ -628,12 +663,13 @@
             dma((high, mates)), dma((high, mates)),
             dma((far,)), dma((far,)),
             dma((max(owners - 1, 1),)), dma((max(owners - 1, 1),)),
+            dma((2,)), dma((2,)),
         ],
         compiler_params=pltpu.CompilerParams(
             collective_id=1, has_side_effects=True, vmem_limit_bytes=56 * 1024 * 1024
         ),
         name="collect",
-    )(terms, gates, bank, own)
+    )(terms, edges, notes, gates, bank, own)
 
 
 def shards(frames, kernels, experts, counts, gate_weights, cotangent):
@@ -669,10 +705,12 @@
     t = lax.axis_index("tile")
     rim = jnp.stack([t > 0, t < tiles - 1]).astype(jnp.int32)
 
-    back, gates, bank_grad = owner(
+    spots = jnp.broadcast_to(places.astype(jnp.float32)[:, :, None], (owners, CAP, 128))
+    spots = jnp.pad(spots, ((0, 0), (0, 8 - CAP), (0, 0)))
+    back, edges, gates, bank_grad = owner(
         pick, shares, places, rim, rows, above, below, kernels, tiles
     )
-    result, input_grad, gated, bank_part = collect(back, gates, bank_grad, own)
+    result, input_grad, gated, bank_part = collect(back, edges, spots, gates, bank_grad, own)
     kernel_part = jnp.swapaxes(bank_part, 1, 2).reshape(
         kernels.shape[:3] + (bank_part.shape[1],)
     )

time: 109 us -> 107 us (0.982)
  Pallas kernels: 95.7 us -> 89.7 us
  local copies, waits for them, and re-layouts: 8.03 us -> 12.3 us
    pallas_call x1, Pallas kernels: 48.9 us -> 43.1 us  [collect(): pl.pallas_call(functools.partial(collect_kernel, deep, across, high, core...]
    unnamed x7 -> x13, local copies, waits for them, and re-layouts: 7.07 us -> 10.7 us
where the time goes in v5:
time: 107 us
  Pallas kernels  89.7 us (84%)
  local copies, waits for them, and re-layouts  12.3 us (11%)
  other arithmetic  4.36 us (4%)
    pallas_call x1, Pallas kernels, collect(): pl.pallas_call(functools.partial(collect_kernel, deep, across, high, core...  43.1 us
    pallas_call x1, Pallas kernels, spread(): pl.pallas_call(functools.partial(spread_kernel, deep, across, tiles), out...  31 us
    pallas_call x1, Pallas kernels, owner(): pl.pallas_call(owner_kernel, grid_spec=spec, out_shape=[jax.ShapeDtypeStr...  15.6 us
    unnamed x13, local copies, waits for them, and re-layouts  10.7 us

profile of v5, /device:TPU:0, one launch (start us, length us, event | category | flops | bytes accessed | tf_op | source)
XLA Modules:
  0.0 107.1 jit_solution(8666162947308008422)
XLA Ops:
  0.6 0.7 add_select_fusion.1
  1.3 0.7 iota_compare_fusion.2
  2.0 0.1 select_reduce_fusion.2
  2.2 0.8 select_reduce_fusion.1
  3.1 0.1 copy.31
  3.2 1.0 pad_maximum_fusion.own_ref
  4.2 31.0 %spread.1 = (bf16[8,2,4,64,256]{4,3,2,1,0:T(8,128)(2,1)S(1)}, bf16[8,4,64,256]{3,2,1,0:T(8,128)(2,1)S(1)}, bf16[8,4,64,256]{3,2,1,0:T(8,128)(2,1)S(1)}, f32[8,8,128]{2,1,0:T(8,128)S(1)}) custom-call(bf16[2,4,64,256]{3,2,1,0:T(8,128)(2,1)S(1)} %pad_maximum_fusion.own_ref, f32[8,8,128]{2,1,0:T(8,128)S(1)} %pad.8.note_ref), custom_call_target="tpu_custom_call" | custom-call | tf_op jit(solution)/shard_map/spread/pallas_call | solution.py:345
  35.2 1.3 %copy-done.1 = bf16[8,2,4,64,256]{4,3,2,1,0:T(8,128)(2,1)} copy-done((bf16[8,2,4,64,256]{4,3,2,1,0:T(8,128)(2,1)}, bf16[8,2,4,64,256]{4,3,2,1,0:T(8,128)(2,1)S(1)}, u32[]{:S(2)}) %copy-start.1) | copy-done | bytes 2097176
  36.5 0.1 fusion.3
  36.6 0.1 convert_reduce_fusion.pick_ref
  36.7 0.1 add_convert_fusion.rim_ref
  36.8 15.6 %owner.1 = (bf16[8,2,4,64,256]{4,3,2,1,0:T(8,128)(2,1)S(1)}, bf16[8,2,2,64,256]{4,3,2,1,0:T(8,128)(2,1)S(1)}, f32[8,8,128]{2,1,0:T(8,128)S(1)}, bf16[4,36,64,256]{3,2,1,0:T(8,128)(2,1)}) custom-call(s32[8]{0:T(128)S(1)} %convert_reduce_fusion.pick_ref, f32[8,2]{1,0:T(8,128)S(1)} %get-tuple-element.46.weight_ref, s32[8,2]{1,0:T(8,128)S(1)} %get-tuple-element.45.place_ref, ...), custom_call_target="tpu_custom_call" | custom-call | tf_op jit(solution)/shard_map/owner/pallas_call | solution.py:146
  52.4 1.3 %copy-done.2 = bf16[8,2,4,64,256]{4,3,2,1,0:T(8,128)(2,1)} copy-done((bf16[8,2,4,64,256]{4,3,2,1,0:T(8,128)(2,1)}, bf16[8,2,4,64,256]{4,3,2,1,0:T(8,128)(2,1)S(1)}, u32[]{:S(2)}) %copy-start.2) | copy-done | bytes 2097176
  53.7 1.0 copy-done.3
  54.7 0.6 copy-done.4
  55.3 0.1 broadcast_in_dim.112
  55.4 0.6 pad.9.note_ref
  56.0 43.1 %collect.1 = (bf16[4,64,256]{2,1,0:T(8,128)(2,1)}, bf16[4,64,256]{2,1,0:T(8,128)(2,1)}, f32[8,8,128]{2,1,0:T(8,128)}, f32[36,64,256]{2,1,0:T(8,128)}) custom-call(bf16[8,2,4,64,256]{4,3,2,1,0:T(8,128)(2,1)} %copy-done.2, bf16[8,2,2,64,256]{4,3,2,1,0:T(8,128)(2,1)} %copy-done.3, f32[8,8,128]{2,1,0:T(8,128)} %pad.9.note_ref, f32[8,8,128]{2,1,0:T(8,128)} %copy-done.4, ...), custom_call_target="tpu_custom_call" | custom-call | tf_op jit(solution)/shard_map/collect/pallas_call | solution.py:636
  99.1 0.8 slice.19
  99.8 0.1 copy.33
  99.9 0.7 select_reduce_fusion
  100.6 1.6 %copy.42 = bf16[4,1,64,256]{3,2,1,0:T(8,128)(2,1)} copy(bf16[4,1,64,256]{3,2,1,0:T(8,128)(2,1)} %bitcast.33) | data formatting | bytes 262144
  102.2 1.6 %copy.43 = bf16[4,1,64,256]{3,2,1,0:T(8,128)(2,1)} copy(bf16[4,1,64,256]{3,2,1,0:T(8,128)(2,1)} %bitcast.32) | data formatting | bytes 262144
  103.7 3.3 %copy.44 = f32[4,9,256,64]{2,3,1,0:T(8,128)} copy(f32[4,9,256,64]{2,3,1,0:T(8,128)} %bitcast.31) | data formatting | bytes 4718592
  (19 shorter events, 0.2 us)
Async XLA Ops:
  4.2 48.2 %copy-start = (bf16[2,4,64,256]{3,2,1,0:T(8,128)(2,1)}, bf16[2,4,64,256]{3,2,1,0:T(8,128)(2,1)S(1)}, u32[]{:S(2)}) copy-start(bf16[2,4,64,256]{3,2,1,0:T(8,128)(2,1)S(1)} %pad_maximum_fusion.own_ref) | copy-start | bytes 786436
  35.2 1.3 %copy-start.1 = (bf16[8,2,4,64,256]{4,3,2,1,0:T(8,128)(2,1)}, bf16[8,2,4,64,256]{4,3,2,1,0:T(8,128)(2,1)S(1)}, u32[]{:S(2)}) copy-start(bf16[8,2,4,64,256]{4,3,2,1,0:T(8,128)(2,1)S(1)} %get-tuple-element.17.rows_ref) | copy-start | bytes 6291460
  52.4 1.3 %copy-start.2 = (bf16[8,2,4,64,256]{4,3,2,1,0:T(8,128)(2,1)}, bf16[8,2,4,64,256]{4,3,2,1,0:T(8,128)(2,1)S(1)}, u32[]{:S(2)}) copy-start(bf16[8,2,4,64,256]{4,3,2,1,0:T(8,128)(2,1)S(1)} %get-tuple-element.20.terms_ref) | copy-start | bytes 6291460
  53.7 1.0 copy-start.3
  54.7 0.6 copy-start.4
